TPU v7x, 128 devices: a whole 4x4x4 slice. The times are simulated.
128 devices in a mesh: pair: 16 (over y_hi, z, core), aux: 8 (over y_lo, x).
Axes of the slice: x: 4, y: 4 (y_hi: 2, y_lo: 2; y = y_hi * 2 + y_lo), z: 4, core: 2. Of those that a mesh axis runs over, the one named last changes fastest.
Arguments:
- c_occ: bfloat16 [12288, 1024], P('pair', 'aux'), may hold values from -0.1875 to 0.1875
- c_vir: bfloat16 [12288, 11264], P('pair', 'aux'), may hold values from -0.0546875 to 0.0546875
- e_occ: float32 [1024], P('aux'), may hold values from -2 to -0.3
- e_vir: float32 [11264], P('aux'), may hold values from 0.2 to 3
- tau_points: float32 [2], replicated, may hold values from 0.2 to 2
- pair_blocks: int32 [64, 2], P('pair'), may hold values from 0 to 767
- block_count: int32 [16], P('pair'), may hold values from 1 to 4, 40 in all
- three_center: bfloat16 [18432, 64, 256], P('aux', 'pair'), may hold values from -0.59765625 to 0.59765625
Outputs:
- coupling: float32 [18432, 2, 1024], P(('aux', 'pair'))
Inputs may be any that keep to these rules, and one draw needn't show every extreme that they name: pair_blocks[s] names the AO shell blocks of the rows and the columns of slot s. Slots s with s mod 4 < block_count[s // 4] are live, the others are ignored; some index of pair has all 4 slots live.
All inputs are finite; a program needn't handle non-finite values. No bound on the sum of `block_count` on one device may be relied on, other than what follows from the above.
Results may differ from a plain program's by a relative error of at most 0.0046.
Values may be sent and summed in bfloat16 or wider, within the bound.
No kernel may reach another device: no remote copies, remote signals or barrier semaphores. Data moves between devices by JAX's collectives and lax.ppermute only.
A program may use at most 128 MiB of HBM per device.

v0:
```python
import jax
import jax.numpy as jnp
from jax import lax
from jax.experimental import pallas as pl
from jax.experimental.pallas import tpu as pltpu
from jax.sharding import Mesh, PartitionSpec as P

BS = 16
TILE = BS * BS
WIN_DEV = 128
LIVE = 40
OWN = 4
CHIP = 2 * OWN
PAIR = ("yh", "z", "c")
ZY = ("yh", "z")
AUX = ("yl", "x")
SWAP = [(0, 1), (1, 0)]
XP = [(i, (i + 1) % 4) for i in range(4)]
XM = [(i, (i - 1) % 4) for i in range(4)]
F32 = jnp.float32
BF16 = jnp.bfloat16


def shift_zy(i):
    return [(y * 4 + z, ((y + i // 4) % 2) * 4 + (z + i % 4) % 4) for y in range(2) for z in range(4)]


def spread(x, axes, count):
    return lax.all_to_all(jnp.broadcast_to(x[None], (count,) + x.shape), axes, 0, 0)


def moved_kernel(where_ref, bound_ref, tiles_ref, *refs):
    pieces = refs[:16]
    out_ref, acc_ref, eo_ref, ev_ref, oe_ref, ve_ref, win_ref, all_ref, sems = refs[16:]
    copies = [
        pltpu.make_async_copy(piece, all_ref.at[pl.ds(n * OWN, OWN)], sems.at[n])
        for n, piece in enumerate(pieces)
    ]
    for copy in copies:
        copy.start()
    lane = lax.broadcasted_iota(jnp.int32, (128, 2048), 1)
    row = lax.broadcasted_iota(jnp.int32, (128, 2048), 0)
    block = (lane // TILE) * BS
    eo_ref[...] = (row == block + (lane % TILE) // BS).astype(BF16)
    ev_ref[...] = (row == block + lane % BS).astype(BF16)
    acc_ref[...] = jnp.zeros_like(acc_ref)
    for copy in copies:
        copy.wait()

    def group(g, carry):
        at = pl.multiple_of(g * 128, 128)
        occ = tiles_ref[:, 0, :, pl.ds(at, 128)].reshape(128, 128)
        vir = tiles_ref[:, 1, :, pl.ds(at, 128)].reshape(128, 128)
        oe_ref[...] = jnp.dot(occ, eo_ref[...], preferred_element_type=F32)
        ve_ref[...] = jnp.dot(vir, ev_ref[...], preferred_element_type=F32)
        for r in range(8):
            win_ref[r] = all_ref[where_ref[g * 8 + r]].T

        def target(s, c):
            rows = pl.multiple_of(s * BS, BS)
            to = pl.multiple_of(s * TILE, TILE)
            total = acc_ref[pl.ds(to, TILE), :]
            for r in range(8):
                v = ve_ref[pl.ds(rows, BS), r * TILE:(r + 1) * TILE]
                kron = jnp.concatenate(
                    [
                        (oe_ref[pl.ds(rows + i, 1), r * TILE:(r + 1) * TILE] * v).astype(BF16)
                        for i in range(BS)
                    ], axis=0)
                total = total + jnp.dot(kron, win_ref[r], preferred_element_type=F32)
            acc_ref[pl.ds(to, TILE), :] = total
            return c

        carry = lax.fori_loop(0, bound_ref[0], target, carry)
        return lax.fori_loop(OWN, OWN + bound_ref[1], target, carry)

    lax.fori_loop(0, LIVE // 8, group, 0)
    out_ref[...] = acc_ref[...].astype(BF16)


def moved_blocks(where, bounds, tiles, pieces):
    vm = pl.BlockSpec(memory_space=pltpu.VMEM)
    sm = pl.BlockSpec(memory_space=pltpu.SMEM)
    return pl.pallas_call(
        moved_kernel,
        out_shape=jax.ShapeDtypeStruct((CHIP * TILE, WIN_DEV), BF16),
        in_specs=[sm, sm, vm] + [pl.BlockSpec(memory_space=pl.ANY)] * 16,
        out_specs=vm,
        scratch_shapes=[
            pltpu.VMEM((CHIP * TILE, WIN_DEV), F32),
            pltpu.VMEM((128, 2048), BF16),
            pltpu.VMEM((128, 2048), BF16),
            pltpu.VMEM((128, 2048), F32),
            pltpu.VMEM((128, 2048), F32),
            pltpu.VMEM((8, TILE, WIN_DEV), BF16),
            pltpu.VMEM((16 * OWN, WIN_DEV, TILE), BF16),
            pltpu.SemaphoreType.DMA((16,)),
        ],
        name="moved",
    )(where, bounds, tiles, *pieces)


def partial_kernel(dest_ref, mine_ref, other_ref, *refs):
    half = OWN * TILE
    outs = refs[-8:]
    refs = list(refs[:-8])
    step = pl.program_id(0)
    tops = [ref[:half] for ref in refs]
    bots = [ref[half:] for ref in refs]
    values = []
    for n in range(0, len(tops), 2):
        top = jnp.concatenate(tops[n:n + 2], axis=1)
        bot = jnp.concatenate(bots[n:n + 2], axis=1)
        value = jnp.dot(mine_ref[...], top, preferred_element_type=F32)
        value = value + jnp.dot(other_ref[...], bot, preferred_element_type=F32)
        values.append(value.astype(BF16))
    value = jnp.concatenate(values, axis=1)
    rows = outs[0].shape[0]
    for k, out_ref in enumerate(outs):
        for h in range(2):
            @pl.when(dest_ref[k] == 2 * step + h)
            def _():
                out_ref[...] = value[h * rows:(h + 1) * rows]


def partial_rows(dests, mine, other, pieces):
    rows = mine.shape[0] // 8
    a_spec = pl.BlockSpec((2 * rows, mine.shape[1]), lambda i, d: (i, 0))
    vm = pl.BlockSpec(memory_space=pltpu.VMEM)
    return pl.pallas_call(
        partial_kernel,
        out_shape=[jax.ShapeDtypeStruct((rows, 4 * WIN_DEV), BF16)] * 8,
        grid_spec=pltpu.PrefetchScalarGridSpec(
            num_scalar_prefetch=1,
            grid=(4,),
            in_specs=[a_spec, a_spec] + [vm] * len(pieces),
            out_specs=[vm] * 8,
        ),
        name="partial",
    )(dests, mine, other, *pieces)


def finish_kernel(core_ref, place_ref, *refs):
    out_ref = refs[-1]
    first = core_ref[0] == 0
    for b in range(8):
        stay, came = refs[2 * (b // 4)], refs[2 * (b // 4) + 1]
        at = slice((b % 4) * WIN_DEV, (b % 4 + 1) * WIN_DEV)
        s, r = stay[:, at], came[:, at]
        to = pl.multiple_of(place_ref[b] * WIN_DEV, WIN_DEV)
        out_ref[:, 0, pl.ds(to, WIN_DEV)] = jnp.where(first, s, r)
        out_ref[:, 1, pl.ds(to, WIN_DEV)] = jnp.where(first, r, s)


def finish(core, place, parts):
    vm = pl.BlockSpec(memory_space=pltpu.VMEM)
    sm = pl.BlockSpec(memory_space=pltpu.SMEM)
    rows = parts[0].shape[0]
    return pl.pallas_call(
        finish_kernel,
        out_shape=jax.ShapeDtypeStruct((rows, 2, 8 * WIN_DEV), F32),
        in_specs=[sm, sm] + [vm] * 4,
        out_specs=vm,
        name="finish",
    )(core, place, *parts)


def step(c_occ, c_vir, e_occ, e_vir, tau_points, pair_blocks, block_count, three_center):
    y, z, c = lax.axis_index("yh"), lax.axis_index("z"), lax.axis_index("c")
    yl, x = lax.axis_index("yl"), lax.axis_index("x")
    group = (y * 4 + z) * 2 + c
    aux_rows = three_center.shape[0]
    chip_rows = aux_rows // 8

    window = jnp.transpose(three_center[:WIN_DEV], (1, 0, 2))
    near = [window] + [lax.ppermute(window, ZY, shift_zy(i)) for i in range(1, 8)]
    windows = near + [lax.ppermute(piece, "c", SWAP) for piece in near]

    facts = jnp.concatenate([pair_blocks.reshape(-1), block_count])
    facts = jnp.pad(facts, (0, 128 - facts.shape[0]))
    facts = jnp.broadcast_to(facts[None], (8, 128))
    facts = spread(facts, PAIR, 16)
    facts = facts[:, 0]
    names = facts[:, :2 * OWN].reshape(16 * OWN, 2)
    counts = facts[:, 2 * OWN]

    groups = jnp.arange(16, dtype=jnp.int32)
    before = jnp.sum(jnp.where(groups[None, :] < groups[:, None], counts[None, :], 0), axis=1)
    slots = jnp.arange(16 * OWN, dtype=jnp.int32)
    slot_in = slots % OWN
    slot_rank = jnp.where(
        slot_in < jnp.repeat(counts, OWN), jnp.repeat(before, OWN) + slot_in, -1)
    chosen = jnp.arange(LIVE, dtype=jnp.int32)[:, None] == slot_rank[None, :]
    sg = slots // OWN
    place_of = (
        jnp.where(sg % 2 == c, 0, 8 * OWN)
        + (((y - sg // 8) % 2) * 4 + (z - (sg // 2) % 4) % 4) * OWN + slot_in)
    where = jnp.sum(jnp.where(chosen, place_of[None, :], 0), axis=1)
    live_names = jnp.sum(jnp.where(chosen[:, :, None], names[None], 0), axis=1)

    local = jnp.arange(c_occ.shape[0], dtype=jnp.int32)
    wanted = live_names[:, None, :] * BS + jnp.arange(BS, dtype=jnp.int32)[None, :, None]
    wanted = wanted.reshape(LIVE * BS, 2) - group * c_occ.shape[0]
    pick_occ = (wanted[:, :1] == local[None, :]).astype(BF16)
    pick_vir = (wanted[:, 1:] == local[None, :]).astype(BF16)
    rows = jnp.concatenate(
        [
            jnp.dot(pick_occ, c_occ, preferred_element_type=F32).astype(BF16),
            jnp.dot(pick_vir, c_vir, preferred_element_type=F32).astype(BF16),
        ], axis=1)
    n_occ = c_occ.shape[1]
    n_half = rows.shape[1] // 2
    kept = jnp.where(c == 0, rows[:, :n_half], rows[:, n_half:])
    given = jnp.where(c == 0, rows[:, n_half:], rows[:, :n_half])
    base_own = lax.dynamic_index_in_dim(before, group, 0, keepdims=False)
    base_next = lax.dynamic_index_in_dim(before, group + 1 - 2 * c, 0, keepdims=False)
    given = lax.ppermute(given, "c", SWAP)
    given, base_own, base_next = lax.optimization_barrier((given, base_own, base_next))
    kept = kept + given
    kept = lax.all_to_all(kept.reshape(8, -1, n_half), ZY, 0, 0)
    kept = jnp.sum(kept.astype(F32), axis=0).astype(BF16)
    kept = spread(kept, ZY, 8).reshape(LIVE * BS, n_half)
    given = lax.ppermute(kept, "c", SWAP)
    rows = jnp.concatenate(
        [jnp.where(c == 0, kept, given), jnp.where(c == 0, given, kept)], axis=1)

    tau = jnp.where(c == 0, tau_points[0], tau_points[1])
    factor = jnp.concatenate([jnp.exp(tau * e_occ / 2.0), jnp.exp(-tau * e_vir / 2.0)])
    scaled = (rows.astype(F32) * factor[None, :]).astype(BF16)
    padded = jnp.concatenate([scaled, jnp.zeros((OWN * BS, scaled.shape[1]), BF16)], axis=0)
    own = jnp.concatenate(
        [
            lax.dynamic_slice_in_dim(padded, base_own * BS, OWN * BS, 0),
            lax.dynamic_slice_in_dim(padded, base_next * BS, OWN * BS, 0),
        ], axis=0)
    numbers = (((1,), (1,)), ((), ()))
    grams = jnp.stack(
        [
            lax.dot_general(own[:, :n_occ], scaled[:, :n_occ], numbers, preferred_element_type=F32),
            lax.dot_general(own[:, n_occ:], scaled[:, n_occ:], numbers, preferred_element_type=F32),
        ])
    grams = grams.reshape(2, CHIP, BS, LIVE * BS).transpose(1, 0, 2, 3)
    grams, three_center = lax.optimization_barrier((grams, three_center))
    mine = three_center.reshape(aux_rows, OWN * TILE)
    other = lax.ppermute(mine, "c", SWAP)
    grams = jnp.sum(lax.all_to_all(grams, AUX, 0, 0), axis=0)
    grams = grams.astype(BF16)
    tiles = spread(grams, AUX, 8)

    bounds = jnp.stack([
        lax.dynamic_index_in_dim(counts, group, 0, keepdims=False),
        lax.dynamic_index_in_dim(counts, group + 1 - 2 * c, 0, keepdims=False)])
    moved = moved_blocks(where, bounds, tiles, windows)

    by = lax.ppermute(moved, "yl", SWAP)
    bp = lax.ppermute(moved, "x", XP)
    bm = lax.ppermute(moved, "x", XM)
    byp = lax.ppermute(by, "x", XP)
    bym = lax.ppermute(by, "x", XM)
    bpp = lax.ppermute(bp, "x", XP)
    order = (6, 2, 5, 7, 1, 3, 4, 0)
    dests = jnp.stack([((y + i // 4) % 2) * 4 + (z + i % 4) % 4 for i in order]).astype(jnp.int32)
    partials = [partial_rows(dests, mine, other, [moved, by, bp, bm])]
    bym, partials[0] = lax.optimization_barrier((bym, partials[0]))
    bymm = lax.ppermute(bym, "x", XM)
    partials.append(partial_rows(dests, mine, other, [byp, bym, bpp, bymm]))
    yo = 1 - yl
    xp, xm, x2 = (x - 1) % 4, (x + 1) % 4, (x + 2) % 4
    place = jnp.stack([yl * 4 + x, yo * 4 + x, yl * 4 + xp, yl * 4 + xm,
                       yo * 4 + xp, yo * 4 + xm, yl * 4 + x2, yo * 4 + x2]).astype(jnp.int32)
    rows_dev = chip_rows // 2
    ends = []
    for partial in partials:
        sums = []
        for i, part in zip(order, partial):
            sums.append(lax.ppermute(part, ZY, shift_zy(i)) if i else part)
        leave = sum(lax.dynamic_slice_in_dim(part, (1 - c) * rows_dev, rows_dev, 0).astype(F32)
                    for part in sums)
        leave, *sums = lax.optimization_barrier((leave, *sums))
        stay = sum(lax.dynamic_slice_in_dim(part, c * rows_dev, rows_dev, 0).astype(F32)
                   for part in sums)
        ends += [stay, lax.ppermute(leave, "c", SWAP)]
    return finish(c.astype(jnp.int32).reshape(1), place, ends)


def solution(mesh):
    inner = Mesh(mesh.devices.reshape(2, 4, 2, 2, 4), ("yh", "z", "c", "yl", "x"))
    placed = (
        P(PAIR, AUX),
        P(PAIR, AUX),
        P(AUX),
        P(AUX),
        P(),
        P(PAIR, None),
        P(PAIR),
        P(AUX, PAIR, None),
    )
    return jax.shard_map(
        step,
        mesh=inner,
        in_specs=placed,
        out_specs=P(AUX + PAIR, None, None),
        check_vma=False,
    )
```

profile of v0, /device:TPU:0, one launch (start us, length us, event | category | flops | bytes accessed | tf_op | source)
XLA Modules:
  0.0 260.0 jit_solution(12715078771733813251)
XLA Ops:
  0.8 0.8 copy.23
  1.7 0.6 broadcast_in_dim_broadcast_in_dim_broadcast_in_dim.2
  2.4 8.2 %all-to-all-start = ((s32[16,8,128]{2,1,0:T(8,128)}), s32[16,8,128]{2,1,0:T(8,128)S(1)}, u32[]{:S(2)}, u32[]{:S(2)}) async-start(s32[16,8,128]{2,1,0:T(8,128)} %broadcast_in_dim_broadcast_in_dim_broadcast_in_dim.2), calls=%async_computation | async-start | bytes 131072 | tf_op jit(solution)/shard_map/all_to_all | solution.py:29
  10.7 7.6 %all-to-all-done = s32[16,8,128]{2,1,0:T(8,128)S(1)} async-done(((s32[16,8,128]{2,1,0:T(8,128)}), s32[16,8,128]{2,1,0:T(8,128)S(1)}, u32[]{:S(2)}, u32[]{:S(2)}) %all-to-all-start) | async-done | bytes 65568 | tf_op jit(solution)/shard_map/all_to_all | solution.py:29
  19.4 1.5 fusion.3
  21.1 1.7 convolution_convert_fusion
  22.9 1.4 broadcast_select_fusion.2
  24.5 0.6 fusion.24
  25.1 2.1 collective-permute-done
  27.2 1.8 select_add_fusion
  29.0 19.5 %all_to_all.25 = bf16[8,80,768]{2,1,0:T(8,128)(2,1)S(1)} all-to-all(bf16[8,80,768]{2,1,0:T(8,128)(2,1)S(1)} %bitcast.49), channel_id=1, replica_groups=mesh['yh'=2,'z'=4,'c'=2,'yl'=2,'x'=4] {'yh','z'}, dimensions={0} | all-to-all | bytes 1966080 | tf_op jit(solution)/shard_map/all_to_all | solution.py:220
  48.7 19.2 %all_to_all.26 = bf16[8,80,768]{2,1,0:T(8,128)(2,1)S(1)} all-to-all(bf16[8,80,768]{2,1,0:T(8,128)(2,1)S(1)} %broadcast_in_dim.99), channel_id=1, replica_groups=mesh['yh'=2,'z'=4,'c'=2,'yl'=2,'x'=4] {'yh','z'}, dimensions={0} | all-to-all | bytes 1966080 | tf_op jit(solution)/shard_map/all_to_all | solution.py:29
  71.1 1.3 broadcast_select_fusion.1
  72.9 0.7 fusion.1
  73.8 0.9 maximum_bitcast_fusion
  74.8 3.7 %copy.30 = bf16[288,8,4,256]{3,1,2,0:T(8,128)(2,1)} copy(bf16[288,8,4,256]{3,2,1,0:T(4,128)(2,1)S(1)} %bitcast.48) | data formatting | bytes 9437184
  79.6 2.1 collective-permute-start.3
  81.7 1.1 collective-permute-start.4
  82.8 4.5 %all-to-all-start.3 = ((f32[8,2,16,640]{3,2,1,0:T(8,128)}), f32[8,2,16,640]{3,2,1,0:T(8,128)S(1)}, u32[]{:S(2)}, u32[]{:S(2)}) async-start(f32[8,2,16,640]{3,2,1,0:T(8,128)} %maximum_bitcast_fusion), calls=%async_computation.3 | async-start | bytes 1310720 | tf_op jit(solution)/shard_map/all_to_all | solution.py:246
  87.2 1.5 collective-permute-start.5
  88.7 5.6 %collective-permute-done.2.refs_1_ = bf16[4,128,256]{2,1,0:T(8,128)(2,1)S(1)} collective-permute-done((bf16[4,128,256]{2,1,0:T(8,128)(2,1)S(1)}, bf16[4,128,256]{2,1,0:T(8,128)(2,1)S(1)}, u32[]{:S(2)}, u32[]{:S(2)}) %collective-permute-start.2) | collective-permute-done | bytes 262176 | tf_op jit(solution)/shard_map/ppermute | solution.py:176
  94.3 3.4 %collective-permute-start.7 = (bf16[4,128,256]{2,1,0:T(8,128)(2,1)S(1)}, bf16[4,128,256]{2,1,0:T(8,128)(2,1)S(1)}, u32[]{:S(2)}, u32[]{:S(2)}) collective-permute-start(bf16[4,128,256]{2,1,0:T(8,128)(2,1)S(1)} %bitcast.57), channel_id=1, source_target_pairs={{0,96},{16,112},{32,64},{48,80},{64,32},{80,48},{96,0},{112,16},{1... | collective-permute-start | bytes 786440 | tf_op jit(solution)/shard_map/ppermute | solution.py:176
  97.8 2.3 collective-permute-start.8
  100.0 3.0 %collective-permute-done.5.refs_4_ = bf16[4,128,256]{2,1,0:T(8,128)(2,1)S(1)} collective-permute-done((bf16[4,128,256]{2,1,0:T(8,128)(2,1)S(1)}, bf16[4,128,256]{2,1,0:T(8,128)(2,1)S(1)}, u32[]{:S(2)}, u32[]{:S(2)}) %collective-permute-start.5) | collective-permute-done | bytes 262176 | tf_op jit(solution)/shard_map/ppermute | solution.py:176
  103.1 6.2 %collective-permute-done.6.refs_5_ = bf16[4,128,256]{2,1,0:T(8,128)(2,1)S(1)} collective-permute-done((bf16[4,128,256]{2,1,0:T(8,128)(2,1)S(1)}, bf16[4,128,256]{2,1,0:T(8,128)(2,1)S(1)}, u32[]{:S(2)}, u32[]{:S(2)}) %collective-permute-start.6) | collective-permute-done | bytes 262176 | tf_op jit(solution)/shard_map/ppermute | solution.py:176
  109.3 6.7 %collective-permute-done.7.refs_6_ = bf16[4,128,256]{2,1,0:T(8,128)(2,1)S(1)} collective-permute-done((bf16[4,128,256]{2,1,0:T(8,128)(2,1)S(1)}, bf16[4,128,256]{2,1,0:T(8,128)(2,1)S(1)}, u32[]{:S(2)}, u32[]{:S(2)}) %collective-permute-start.7) | collective-permute-done | bytes 262176 | tf_op jit(solution)/shard_map/ppermute | solution.py:176
  116.0 3.2 %collective-permute-done.8.refs_7_ = bf16[4,128,256]{2,1,0:T(8,128)(2,1)S(1)} collective-permute-done((bf16[4,128,256]{2,1,0:T(8,128)(2,1)S(1)}, bf16[4,128,256]{2,1,0:T(8,128)(2,1)S(1)}, u32[]{:S(2)}, u32[]{:S(2)}) %collective-permute-start.8) | collective-permute-done | bytes 262176 | tf_op jit(solution)/shard_map/ppermute | solution.py:176
  119.3 0.7 copy-done.13
  120.0 0.8 broadcast_in_dim.100
  120.7 4.3 %all-to-all-start.4 = ((bf16[8,2,16,640]{3,2,1,0:T(8,128)(2,1)}), bf16[8,2,16,640]{3,2,1,0:T(8,128)(2,1)S(1)}, u32[]{:S(2)}, u32[]{:S(2)}) async-start(bf16[8,2,16,640]{3,2,1,0:T(8,128)(2,1)} %broadcast_in_dim.100), calls=%async_computation.4 | async-start | bytes 655360 | tf_op jit(solution)/shard_map/all_to_all | solution.py:29
  126.7 1.9 pad_add_fusion.1.bound_ref
  128.5 0.7 select_reduce_fusion.1.where_ref
  129.3 0.7 copy-done.16
  130.0 3.6 %all-to-all-done.4.tiles_ref = bf16[8,2,16,640]{3,2,1,0:T(8,128)(2,1)S(1)} async-done(((bf16[8,2,16,640]{3,2,1,0:T(8,128)(2,1)}), bf16[8,2,16,640]{3,2,1,0:T(8,128)(2,1)S(1)}, u32[]{:S(2)}, u32[]{:S(2)}) %all-to-all-start.4) | async-done | bytes 327712 | tf_op jit(solution)/shard_map/all_to_all | solution.py:29
  133.7 0.7 copy-done.2
  134.4 14.7 %moved.1.refs_0_ = bf16[2048,128]{1,0:T(8,128)(2,1)} custom-call(s32[40]{0:T(128)} %select_reduce_fusion.1.where_ref, s32[2]{0:T(128)} %pad_add_fusion.1.bound_ref, bf16[8,2,16,640]{3,2,1,0:T(8,128)(2,1)} %copy-done.2, bf16[4,128,256]{2,1,0:T(8,128)(2,1)} %bitcast.60, bf16[4,128,256]{2,1,0:T(8,128)(2,1)} %copy-done.9, ...), custom_call_target="tpu_custom_call" | custom-call | tf_op jit(solution)/shard_map/moved/pallas_call | solution.py:84
  149.8 0.9 collective-permute-start.20
  150.7 2.4 collective-permute-start.21
  153.0 10.1 %collective-permute-done.17.refs_1_ = bf16[2048,128]{1,0:T(8,128)(2,1)} collective-permute-done((bf16[2048,128]{1,0:T(8,128)(2,1)}, bf16[2048,128]{1,0:T(8,128)(2,1)}, u32[]{:S(2)}, u32[]{:S(2)}) %collective-permute-start.17) | collective-permute-done | bytes 524320 | tf_op jit(solution)/shard_map/ppermute | solution.py:255
  163.3 1.9 collective-permute-start.30
  166.0 10.6 %partial.2 = (bf16[288,512]{1,0:T(8,128)(2,1)}, bf16[288,512]{1,0:T(8,128)(2,1)}, bf16[288,512]{1,0:T(8,128)(2,1)}, bf16[288,512]{1,0:T(8,128)(2,1)}, bf16[288,5...) custom-call(s32[8]{0:T(128)} %stack.89.dest_ref, ...), custom_call_target="tpu_custom_call" | custom-call | tf_op jit(solution)/shard_map/partial/pallas_call | solution.py:130
  176.6 3.1 %collective-permute-start.32 = (bf16[2048,128]{1,0:T(8,128)(2,1)S(1)}, bf16[2048,128]{1,0:T(8,128)(2,1)S(1)}, u32[]{:S(2)}, u32[]{:S(2)}) collective-permute-start(bf16[2048,128]{1,0:T(8,128)(2,1)S(1)} %collective-permute-done.18.refs_1_), channel_id=1, source_target_pairs={{0,3},{1,0},{2,1},{3,2},{4,7},{5,4},{6,5},{7,6},{8,11},{9,8},{10,9... | collective-permute-start | bytes 1572872 | tf_op jit(solution)/shard_map/ppermute | solution.py:265
  179.8 9.5 %collective-permute-start.28 = (bf16[288,512]{1,0:T(8,128)(2,1)}, bf16[288,512]{1,0:T(8,128)(2,1)}, u32[]{:S(2)}, u32[]{:S(2)}) collective-permute-start(bf16[288,512]{1,0:T(8,128)(2,1)} %get-tuple-element.72), channel_id=1, source_target_pairs={{0,64},{16,80},{32,96},{48,112},{64,0},{80,16},{96,32},{112,48},{1... | collective-permute-start | bytes 884744 | tf_op jit(solution)/shard_map/ppermute | solution.py:276
  189.3 2.0 collective-permute-start.26
  191.3 2.5 collective-permute-start.25
  193.8 0.8 copy-done.6
  194.6 1.9 collective-permute-start.24
  196.6 10.7 %partial.3 = (bf16[288,512]{1,0:T(8,128)(2,1)}, bf16[288,512]{1,0:T(8,128)(2,1)}, bf16[288,512]{1,0:T(8,128)(2,1)}, bf16[288,512]{1,0:T(8,128)(2,1)}, bf16[288,5...) custom-call(s32[8]{0:T(128)} %stack.89.dest_ref, ...), custom_call_target="tpu_custom_call" | custom-call | tf_op jit(solution)/shard_map/partial/pallas_call | solution.py:130
  207.2 5.2 %collective-permute-start.23 = (bf16[288,512]{1,0:T(8,128)(2,1)}, bf16[288,512]{1,0:T(8,128)(2,1)S(1)}, u32[]{:S(2)}, u32[]{:S(2)}) collective-permute-start(bf16[288,512]{1,0:T(8,128)(2,1)} %get-tuple-element.67), channel_id=1, source_target_pairs={{0,32},{16,48},{32,0},{48,16},{64,96},{80,112},{96,64},{112,80},{1... | collective-permute-start | bytes 884744 | tf_op jit(solution)/shard_map/ppermute | solution.py:276
  212.5 4.6 %collective-permute-start.22 = (bf16[288,512]{1,0:T(8,128)(2,1)}, bf16[288,512]{1,0:T(8,128)(2,1)S(1)}, u32[]{:S(2)}, u32[]{:S(2)}) collective-permute-start(bf16[288,512]{1,0:T(8,128)(2,1)} %get-tuple-element.66), channel_id=1, source_target_pairs={{0,96},{16,112},{32,64},{48,80},{64,32},{80,48},{96,0},{112,16},{1... | collective-permute-start | bytes 884744 | tf_op jit(solution)/shard_map/ppermute | solution.py:276
  217.1 2.3 collective-permute-start.38
  219.4 6.0 %collective-permute-done.23 = bf16[288,512]{1,0:T(8,128)(2,1)S(1)} collective-permute-done((bf16[288,512]{1,0:T(8,128)(2,1)}, bf16[288,512]{1,0:T(8,128)(2,1)S(1)}, u32[]{:S(2)}, u32[]{:S(2)}) %collective-permute-start.23) | collective-permute-done | bytes 294944 | tf_op jit(solution)/shard_map/ppermute | solution.py:276
  225.4 3.0 %collective-permute-start.36 = (bf16[288,512]{1,0:T(8,128)(2,1)}, bf16[288,512]{1,0:T(8,128)(2,1)}, u32[]{:S(2)}, u32[]{:S(2)}) collective-permute-start(bf16[288,512]{1,0:T(8,128)(2,1)} %get-tuple-element.87), channel_id=1, source_target_pairs={{0,112},{16,64},{32,80},{48,96},{64,48},{80,0},{96,16},{112,32},{1... | collective-permute-start | bytes 884744 | tf_op jit(solution)/shard_map/ppermute | solution.py:276
  228.4 1.7 collective-permute-start.35
  230.1 1.0 collective-permute-done.39
  231.2 2.6 %collective-permute-start.34 = (bf16[288,512]{1,0:T(8,128)(2,1)}, bf16[288,512]{1,0:T(8,128)(2,1)}, u32[]{:S(2)}, u32[]{:S(2)}) collective-permute-start(bf16[288,512]{1,0:T(8,128)(2,1)} %get-tuple-element.85), channel_id=1, source_target_pairs={{0,32},{16,48},{32,0},{48,16},{64,96},{80,112},{96,64},{112,80},{1... | collective-permute-start | bytes 884744 | tf_op jit(solution)/shard_map/ppermute | solution.py:276
  233.8 6.7 %collective-permute-done.38 = bf16[288,512]{1,0:T(8,128)(2,1)} collective-permute-done((bf16[288,512]{1,0:T(8,128)(2,1)}, bf16[288,512]{1,0:T(8,128)(2,1)}, u32[]{:S(2)}, u32[]{:S(2)}) %collective-permute-start.38) | collective-permute-done | bytes 294944 | tf_op jit(solution)/shard_map/ppermute | solution.py:276
  240.8 2.1 convert_add_fusion.3
  242.9 1.3 collective-permute-done.35
  244.2 7.2 %collective-permute-done.34 = bf16[288,512]{1,0:T(8,128)(2,1)} collective-permute-done((bf16[288,512]{1,0:T(8,128)(2,1)}, bf16[288,512]{1,0:T(8,128)(2,1)}, u32[]{:S(2)}, u32[]{:S(2)}) %collective-permute-start.34) | collective-permute-done | bytes 294944 | tf_op jit(solution)/shard_map/ppermute | solution.py:276
  251.4 2.2 convert_add_fusion.1
  253.7 0.7 stack.76.place_ref
  254.3 2.6 %convert_add_fusion = (f32[144,512]{1,0:T(8,128)}, f32[144,512]{1,0:T(8,128)}) fusion(bf16[288,512]{1,0:T(8,128)(2,1)S(1)} %copy-done.8, s32[]{:T(128)S(6)} %select_n.271, bf16[288,512]{1,0:T(8,128)(2,1)} %collective-permute-done.39, bf16[288,512]{1,0:T(8,128)(2,1)} %collective-permute-done.38, bf16[288,512]{1,0:T(8,128)(2,1)} %collective-permute-done.37, ...), kind=kLoop, calls=%fused_computation.20 | loop fusion | flops 2211840 | bytes 2949124 | tf_op jit(solution)/shard_map/add | solution.py:280
  257.0 3.0 %finish.1 = f32[144,2,1024]{2,1,0:T(2,128)} custom-call(s32[1]{0:T(128)} %bitcast.core_ref, s32[8]{0:T(128)} %stack.76.place_ref, f32[144,512]{1,0:T(8,128)} %get-tuple-element.116.refs_0_, f32[144,512]{1,0:T(8,128)} %collective-permute-done.29.refs_1_, f32[144,512]{1,0:T(8,128)} %get-tuple-element.115.refs_2_, f32[144,512]{1,0:T(8,128)} %collective-permute-done.40.refs_3_), custom_call_target="tpu_custom_call" | custom-call | tf_op jit(solution)/shard_map/finish/pallas_call | solution.py:159
  (131 shorter events, 8.2 us)
Async XLA Ops:
  0.0 21.1 %copy-start = (bf16[768,1408]{1,0:T(8,128)(2,1)S(1)}, bf16[768,1408]{1,0:T(8,128)(2,1)}, u32[]{:S(2)}) copy-start(bf16[768,1408]{1,0:T(8,128)(2,1)} %param.9) | copy-start | bytes 6488068
  2.4 15.8 %all-to-all-start = ((s32[16,8,128]{2,1,0:T(8,128)}), s32[16,8,128]{2,1,0:T(8,128)S(1)}, u32[]{:S(2)}, u32[]{:S(2)}) async-start(s32[16,8,128]{2,1,0:T(8,128)} %broadcast_in_dim_broadcast_in_dim_broadcast_in_dim.2), calls=%async_computation | async-start | bytes 131072 | tf_op jit(solution)/shard_map/all_to_all | solution.py:29
  22.8 1.6 copy-start.1
  24.4 2.8 %collective-permute-start = (bf16[640,768]{1,0:T(8,128)(2,1)}, bf16[640,768]{1,0:T(8,128)(2,1)S(1)}, u32[]{:S(2)}, u32[]{:S(2)}) collective-permute-start(bf16[640,768]{1,0:T(8,128)(2,1)} %broadcast_select_fusion.2), channel_id=1, source_target_pairs={{0,8},{8,0},{1,9},{9,1},{2,10},{10,2},{3,11},{11,3},{4,12},{12,4},... | collective-permute-start | bytes 2949128 | tf_op jit(solution)/shard_map/ppermute | solution.py:217
  48.5 19.4 %copy-start.18 = (f32[2]{0:T(128)S(1)}, f32[2]{0:T(128)}, u32[]{:S(2)}) copy-start(f32[2]{0:T(128)} %param.12) | copy-start | bytes 28
  48.5 21.2 %copy-start.19 = (f32[128]{0:T(128)S(1)}, f32[128]{0:T(128)}, u32[]{:S(2)}) copy-start(f32[128]{0:T(128)} %param.10) | copy-start | bytes 1540
  48.5 21.3 %copy-start.17 = (f32[1408]{0:T(1024)S(1)}, f32[1408]{0:T(1024)}, u32[]{:S(2)}) copy-start(f32[1408]{0:T(1024)} %param.11) | copy-start | bytes 16900
  67.9 3.2 %collective-permute-start.1 = (bf16[640,768]{1,0:T(8,128)(2,1)S(1)}, bf16[640,768]{1,0:T(8,128)(2,1)}, u32[]{:S(2)}, u32[]{:S(2)}) collective-permute-start(bf16[640,768]{1,0:T(8,128)(2,1)S(1)} %bitcast.50), channel_id=1, source_target_pairs={{0,8},{8,0},{1,9},{9,1},{2,10},{10,2},{3,11},{11,3},{4,12},{12,4},... | collective-permute-start | bytes 2949128 | tf_op jit(solution)/shard_map/ppermute | solution.py:223
  72.4 2.3 slice-start
  72.8 2.0 slice-start.1
  78.6 87.4 %collective-permute-start.19 = (bf16[2304,1024]{1,0:T(8,128)(2,1)}, bf16[2304,1024]{1,0:T(8,128)(2,1)}, u32[]{:S(2)}, u32[]{:S(2)}) collective-permute-start(bf16[2304,1024]{1,0:T(8,128)(2,1)} %bitcast.36.mine_ref), channel_id=1, source_target_pairs={{0,8},{8,0},{1,9},{9,1},{2,10},{10,2},{3,11},{11,3},{4,12},{12,4},... | collective-permute-start | bytes 14155784 | tf_op jit(solution)/shard_map/ppermute | solution.py:245
  79.2 54.5 %copy-start.3 = (bf16[128,4,256]{2,0,1:T(8,128)(2,1)}, bf16[128,4,256]{2,0,1:T(8,128)(2,1)S(1)}, u32[]{:S(2)}) copy-start(bf16[128,4,256]{2,0,1:T(8,128)(2,1)S(1)} %copy.32) | copy-start | bytes 786436
  79.2 15.1 %collective-permute-start.2 = (bf16[4,128,256]{2,1,0:T(8,128)(2,1)S(1)}, bf16[4,128,256]{2,1,0:T(8,128)(2,1)S(1)}, u32[]{:S(2)}, u32[]{:S(2)}) collective-permute-start(bf16[4,128,256]{2,1,0:T(8,128)(2,1)S(1)} %bitcast.52), channel_id=1, source_target_pairs={{0,16},{16,32},{32,48},{48,0},{64,80},{80,96},{96,112},{112,64},{1... | collective-permute-start | bytes 786440 | tf_op jit(solution)/shard_map/ppermute | solution.py:176
  79.6 14.7 %collective-permute-start.3 = (bf16[4,128,256]{2,1,0:T(8,128)(2,1)S(1)}, bf16[4,128,256]{2,1,0:T(8,128)(2,1)}, u32[]{:S(2)}, u32[]{:S(2)}) collective-permute-start(bf16[4,128,256]{2,1,0:T(8,128)(2,1)S(1)} %bitcast.53), channel_id=1, source_target_pairs={{0,32},{16,48},{32,0},{48,16},{64,96},{80,112},{96,64},{112,80},{1... | collective-permute-start | bytes 786440 | tf_op jit(solution)/shard_map/ppermute | solution.py:176
  81.7 16.1 %collective-permute-start.4 = (bf16[4,128,256]{2,1,0:T(8,128)(2,1)S(1)}, bf16[4,128,256]{2,1,0:T(8,128)(2,1)}, u32[]{:S(2)}, u32[]{:S(2)}) collective-permute-start(bf16[4,128,256]{2,1,0:T(8,128)(2,1)S(1)} %bitcast.54), channel_id=1, source_target_pairs={{0,48},{16,0},{32,16},{48,32},{64,112},{80,64},{96,80},{112,96},{1... | collective-permute-start | bytes 786440 | tf_op jit(solution)/shard_map/ppermute | solution.py:176
  82.8 37.2 %all-to-all-start.3 = ((f32[8,2,16,640]{3,2,1,0:T(8,128)}), f32[8,2,16,640]{3,2,1,0:T(8,128)S(1)}, u32[]{:S(2)}, u32[]{:S(2)}) async-start(f32[8,2,16,640]{3,2,1,0:T(8,128)} %maximum_bitcast_fusion), calls=%async_computation.3 | async-start | bytes 1310720 | tf_op jit(solution)/shard_map/all_to_all | solution.py:246
  87.2 15.8 %collective-permute-start.5 = (bf16[4,128,256]{2,1,0:T(8,128)(2,1)S(1)}, bf16[4,128,256]{2,1,0:T(8,128)(2,1)S(1)}, u32[]{:S(2)}, u32[]{:S(2)}) collective-permute-start(bf16[4,128,256]{2,1,0:T(8,128)(2,1)S(1)} %bitcast.55), channel_id=1, source_target_pairs={{0,64},{16,80},{32,96},{48,112},{64,0},{80,16},{96,32},{112,48},{1... | collective-permute-start | bytes 786440 | tf_op jit(solution)/shard_map/ppermute | solution.py:176
  94.3 39.3 %copy-start.9 = (bf16[4,128,256]{2,1,0:T(8,128)(2,1)}, bf16[4,128,256]{2,1,0:T(8,128)(2,1)S(1)}, u32[]{:S(2)}) copy-start(bf16[4,128,256]{2,1,0:T(8,128)(2,1)S(1)} %collective-permute-done.2.refs_1_) | copy-start | bytes 786436
  94.3 14.9 %collective-permute-start.6 = (bf16[4,128,256]{2,1,0:T(8,128)(2,1)S(1)}, bf16[4,128,256]{2,1,0:T(8,128)(2,1)S(1)}, u32[]{:S(2)}, u32[]{:S(2)}) collective-permute-start(bf16[4,128,256]{2,1,0:T(8,128)(2,1)S(1)} %bitcast.56), channel_id=1, source_target_pairs={{0,80},{16,96},{32,112},{48,64},{64,16},{80,32},{96,48},{112,0},{1... | collective-permute-start | bytes 786440 | tf_op jit(solution)/shard_map/ppermute | solution.py:176
  94.3 21.7 %collective-permute-start.7 = (bf16[4,128,256]{2,1,0:T(8,128)(2,1)S(1)}, bf16[4,128,256]{2,1,0:T(8,128)(2,1)S(1)}, u32[]{:S(2)}, u32[]{:S(2)}) collective-permute-start(bf16[4,128,256]{2,1,0:T(8,128)(2,1)S(1)} %bitcast.57), channel_id=1, source_target_pairs={{0,96},{16,112},{32,64},{48,80},{64,32},{80,48},{96,0},{112,16},{1... | collective-permute-start | bytes 786440 | tf_op jit(solution)/shard_map/ppermute | solution.py:176
  97.8 21.5 %collective-permute-start.8 = (bf16[4,128,256]{2,1,0:T(8,128)(2,1)S(1)}, bf16[4,128,256]{2,1,0:T(8,128)(2,1)S(1)}, u32[]{:S(2)}, u32[]{:S(2)}) collective-permute-start(bf16[4,128,256]{2,1,0:T(8,128)(2,1)S(1)} %bitcast.58), channel_id=1, source_target_pairs={{0,112},{16,64},{32,80},{48,96},{64,48},{80,0},{96,16},{112,32},{1... | collective-permute-start | bytes 786440 | tf_op jit(solution)/shard_map/ppermute | solution.py:176
  103.1 16.2 %copy-start.10 = (bf16[4,128,256]{2,1,0:T(8,128)(2,1)}, bf16[4,128,256]{2,1,0:T(8,128)(2,1)S(1)}, u32[]{:S(2)}) copy-start(bf16[4,128,256]{2,1,0:T(8,128)(2,1)S(1)} %collective-permute-done.5.refs_4_) | copy-start | bytes 786436
  103.1 21.9 %collective-permute-start.9 = (bf16[4,128,256]{2,1,0:T(8,128)(2,1)S(1)}, bf16[4,128,256]{2,1,0:T(8,128)(2,1)}, u32[]{:S(2)}, u32[]{:S(2)}) collective-permute-start(bf16[4,128,256]{2,1,0:T(8,128)(2,1)S(1)} %bitcast.59), channel_id=1, source_target_pairs={{0,8},{8,0},{1,9},{9,1},{2,10},{10,2},{3,11},{11,3},{4,12},{12,4},... | collective-permute-start | bytes 786440 | tf_op jit(solution)/shard_map/ppermute | solution.py:177
  109.2 10.0 %copy-start.11 = (bf16[4,128,256]{2,1,0:T(8,128)(2,1)}, bf16[4,128,256]{2,1,0:T(8,128)(2,1)S(1)}, u32[]{:S(2)}) copy-start(bf16[4,128,256]{2,1,0:T(8,128)(2,1)S(1)} %collective-permute-done.6.refs_5_) | copy-start | bytes 786436
  109.2 16.1 %collective-permute-start.10 = (bf16[4,128,256]{2,1,0:T(8,128)(2,1)S(1)}, bf16[4,128,256]{2,1,0:T(8,128)(2,1)}, u32[]{:S(2)}, u32[]{:S(2)}) collective-permute-start(bf16[4,128,256]{2,1,0:T(8,128)(2,1)S(1)} %collective-permute-done.2.refs_1_), channel_id=1, source_target_pairs={{0,8},{8,0},{1,9},{9,1},{2,10},{10,2},{3,11},{11,3},{4,12},{12,4},... | collective-permute-start | bytes 786440 | tf_op jit(solution)/shard_map/ppermute | solution.py:177
  116.0 3.2 %copy-start.12 = (bf16[4,128,256]{2,1,0:T(8,128)(2,1)}, bf16[4,128,256]{2,1,0:T(8,128)(2,1)S(1)}, u32[]{:S(2)}) copy-start(bf16[4,128,256]{2,1,0:T(8,128)(2,1)S(1)} %collective-permute-done.7.refs_6_) | copy-start | bytes 786436
  116.0 9.6 %collective-permute-start.11 = (bf16[4,128,256]{2,1,0:T(8,128)(2,1)}, bf16[4,128,256]{2,1,0:T(8,128)(2,1)}, u32[]{:S(2)}, u32[]{:S(2)}) collective-permute-start(bf16[4,128,256]{2,1,0:T(8,128)(2,1)} %collective-permute-done.3.refs_2_), channel_id=1, source_target_pairs={{0,8},{8,0},{1,9},{9,1},{2,10},{10,2},{3,11},{11,3},{4,12},{12,4},... | collective-permute-start | bytes 786440 | tf_op jit(solution)/shard_map/ppermute | solution.py:177
  119.9 5.9 %collective-permute-start.12 = (bf16[4,128,256]{2,1,0:T(8,128)(2,1)}, bf16[4,128,256]{2,1,0:T(8,128)(2,1)}, u32[]{:S(2)}, u32[]{:S(2)}) collective-permute-start(bf16[4,128,256]{2,1,0:T(8,128)(2,1)} %collective-permute-done.4.refs_3_), channel_id=1, source_target_pairs={{0,8},{8,0},{1,9},{9,1},{2,10},{10,2},{3,11},{11,3},{4,12},{12,4},... | collective-permute-start | bytes 786440 | tf_op jit(solution)/shard_map/ppermute | solution.py:177
  120.7 12.9 %all-to-all-start.4 = ((bf16[8,2,16,640]{3,2,1,0:T(8,128)(2,1)}), bf16[8,2,16,640]{3,2,1,0:T(8,128)(2,1)S(1)}, u32[]{:S(2)}, u32[]{:S(2)}) async-start(bf16[8,2,16,640]{3,2,1,0:T(8,128)(2,1)} %broadcast_in_dim.100), calls=%async_computation.4 | async-start | bytes 655360 | tf_op jit(solution)/shard_map/all_to_all | solution.py:29
  125.0 4.2 %collective-permute-start.13 = (bf16[4,128,256]{2,1,0:T(8,128)(2,1)}, bf16[4,128,256]{2,1,0:T(8,128)(2,1)S(1)}, u32[]{:S(2)}, u32[]{:S(2)}) collective-permute-start(bf16[4,128,256]{2,1,0:T(8,128)(2,1)} %copy-done.10), channel_id=1, source_target_pairs={{0,8},{8,0},{1,9},{9,1},{2,10},{10,2},{3,11},{11,3},{4,12},{12,4},... | collective-permute-start | bytes 786440 | tf_op jit(solution)/shard_map/ppermute | solution.py:177
  125.3 3.9 %collective-permute-start.14 = (bf16[4,128,256]{2,1,0:T(8,128)(2,1)}, bf16[4,128,256]{2,1,0:T(8,128)(2,1)S(1)}, u32[]{:S(2)}, u32[]{:S(2)}) collective-permute-start(bf16[4,128,256]{2,1,0:T(8,128)(2,1)} %copy-done.11), channel_id=1, source_target_pairs={{0,8},{8,0},{1,9},{9,1},{2,10},{10,2},{3,11},{11,3},{4,12},{12,4},... | collective-permute-start | bytes 786440 | tf_op jit(solution)/shard_map/ppermute | solution.py:177
  125.6 3.7 %collective-permute-start.15 = (bf16[4,128,256]{2,1,0:T(8,128)(2,1)}, bf16[4,128,256]{2,1,0:T(8,128)(2,1)S(1)}, u32[]{:S(2)}, u32[]{:S(2)}) collective-permute-start(bf16[4,128,256]{2,1,0:T(8,128)(2,1)} %copy-done.12), channel_id=1, source_target_pairs={{0,8},{8,0},{1,9},{9,1},{2,10},{10,2},{3,11},{11,3},{4,12},{12,4},... | collective-permute-start | bytes 786440 | tf_op jit(solution)/shard_map/ppermute | solution.py:177
  125.9 4.1 %collective-permute-start.16 = (bf16[4,128,256]{2,1,0:T(8,128)(2,1)}, bf16[4,128,256]{2,1,0:T(8,128)(2,1)}, u32[]{:S(2)}, u32[]{:S(2)}) collective-permute-start(bf16[4,128,256]{2,1,0:T(8,128)(2,1)} %copy-done.13), channel_id=1, source_target_pairs={{0,8},{8,0},{1,9},{9,1},{2,10},{10,2},{3,11},{11,3},{4,12},{12,4},... | collective-permute-start | bytes 786440 | tf_op jit(solution)/shard_map/ppermute | solution.py:177
  129.3 4.4 %copy-start.14 = (bf16[4,128,256]{2,1,0:T(8,128)(2,1)}, bf16[4,128,256]{2,1,0:T(8,128)(2,1)S(1)}, u32[]{:S(2)}) copy-start(bf16[4,128,256]{2,1,0:T(8,128)(2,1)S(1)} %collective-permute-done.13.refs_12_) | copy-start | bytes 786436
  129.3 4.4 %copy-start.15 = (bf16[4,128,256]{2,1,0:T(8,128)(2,1)}, bf16[4,128,256]{2,1,0:T(8,128)(2,1)S(1)}, u32[]{:S(2)}) copy-start(bf16[4,128,256]{2,1,0:T(8,128)(2,1)S(1)} %collective-permute-done.14.refs_13_) | copy-start | bytes 786436
  133.7 0.7 copy-start.2
  149.2 14.0 %collective-permute-start.17 = (bf16[2048,128]{1,0:T(8,128)(2,1)}, bf16[2048,128]{1,0:T(8,128)(2,1)}, u32[]{:S(2)}, u32[]{:S(2)}) collective-permute-start(bf16[2048,128]{1,0:T(8,128)(2,1)} %moved.1.refs_0_), channel_id=1, source_target_pairs={{0,4},{4,0},{1,5},{5,1},{2,6},{6,2},{3,7},{7,3},{8,12},{12,8},{9,1... | collective-permute-start | bytes 1572872 | tf_op jit(solution)/shard_map/ppermute | solution.py:255
  149.8 15.4 %collective-permute-start.20 = (bf16[2048,128]{1,0:T(8,128)(2,1)}, bf16[2048,128]{1,0:T(8,128)(2,1)}, u32[]{:S(2)}, u32[]{:S(2)}) collective-permute-start(bf16[2048,128]{1,0:T(8,128)(2,1)} %moved.1.refs_0_), channel_id=1, source_target_pairs={{0,1},{1,2},{2,3},{3,0},{4,5},{5,6},{6,7},{7,4},{8,9},{9,10},{10,1... | collective-permute-start | bytes 1572872 | tf_op jit(solution)/shard_map/ppermute | solution.py:256
  150.7 15.3 %collective-permute-start.21 = (bf16[2048,128]{1,0:T(8,128)(2,1)}, bf16[2048,128]{1,0:T(8,128)(2,1)}, u32[]{:S(2)}, u32[]{:S(2)}) collective-permute-start(bf16[2048,128]{1,0:T(8,128)(2,1)} %moved.1.refs_0_), channel_id=1, source_target_pairs={{0,3},{1,0},{2,1},{3,2},{4,7},{5,4},{6,5},{7,6},{8,11},{9,8},{10,9... | collective-permute-start | bytes 1572872 | tf_op jit(solution)/shard_map/ppermute | solution.py:257
  163.1 13.5 %collective-permute-start.18 = (bf16[2048,128]{1,0:T(8,128)(2,1)}, bf16[2048,128]{1,0:T(8,128)(2,1)S(1)}, u32[]{:S(2)}, u32[]{:S(2)}) collective-permute-start(bf16[2048,128]{1,0:T(8,128)(2,1)} %collective-permute-done.17.refs_1_), channel_id=1, source_target_pairs={{0,3},{1,0},{2,1},{3,2},{4,7},{5,4},{6,5},{7,6},{8,11},{9,8},{10,9... | collective-permute-start | bytes 1572872 | tf_op jit(solution)/shard_map/ppermute | solution.py:259
  163.3 26.0 %collective-permute-start.30 = (bf16[2048,128]{1,0:T(8,128)(2,1)}, bf16[2048,128]{1,0:T(8,128)(2,1)S(1)}, u32[]{:S(2)}, u32[]{:S(2)}) collective-permute-start(bf16[2048,128]{1,0:T(8,128)(2,1)} %collective-permute-done.17.refs_1_), channel_id=1, source_target_pairs={{0,1},{1,2},{2,3},{3,0},{4,5},{5,6},{6,7},{7,4},{8,9},{9,10},{10,1... | collective-permute-start | bytes 1572872 | tf_op jit(solution)/shard_map/ppermute | solution.py:258
  165.2 26.1 %collective-permute-start.31 = (bf16[2048,128]{1,0:T(8,128)(2,1)}, bf16[2048,128]{1,0:T(8,128)(2,1)}, u32[]{:S(2)}, u32[]{:S(2)}) collective-permute-start(bf16[2048,128]{1,0:T(8,128)(2,1)} %collective-permute-done.20.refs_2_), channel_id=1, source_target_pairs={{0,1},{1,2},{2,3},{3,0},{4,5},{5,6},{6,7},{7,4},{8,9},{9,10},{10,1... | collective-permute-start | bytes 1572872 | tf_op jit(solution)/shard_map/ppermute | solution.py:260
  176.6 19.9 %copy-start.4 = (bf16[2048,128]{1,0:T(8,128)(2,1)}, bf16[2048,128]{1,0:T(8,128)(2,1)S(1)}, u32[]{:S(2)}) copy-start(bf16[2048,128]{1,0:T(8,128)(2,1)S(1)} %collective-permute-done.18.refs_1_) | copy-start | bytes 1572868
  176.6 64.2 %copy-start.7 = (bf16[288,512]{1,0:T(8,128)(2,1)S(1)}, bf16[288,512]{1,0:T(8,128)(2,1)}, u32[]{:S(2)}) copy-start(bf16[288,512]{1,0:T(8,128)(2,1)} %get-tuple-element.81) | copy-start | bytes 884740
  176.6 17.2 %collective-permute-start.32 = (bf16[2048,128]{1,0:T(8,128)(2,1)S(1)}, bf16[2048,128]{1,0:T(8,128)(2,1)S(1)}, u32[]{:S(2)}, u32[]{:S(2)}) collective-permute-start(bf16[2048,128]{1,0:T(8,128)(2,1)S(1)} %collective-permute-done.18.refs_1_), channel_id=1, source_target_pairs={{0,3},{1,0},{2,1},{3,2},{4,7},{5,4},{6,5},{7,6},{8,11},{9,8},{10,9... | collective-permute-start | bytes 1572872 | tf_op jit(solution)/shard_map/ppermute | solution.py:265
  179.8 27.5 %collective-permute-start.28 = (bf16[288,512]{1,0:T(8,128)(2,1)}, bf16[288,512]{1,0:T(8,128)(2,1)}, u32[]{:S(2)}, u32[]{:S(2)}) collective-permute-start(bf16[288,512]{1,0:T(8,128)(2,1)} %get-tuple-element.72), channel_id=1, source_target_pairs={{0,64},{16,80},{32,96},{48,112},{64,0},{80,16},{96,32},{112,48},{1... | collective-permute-start | bytes 884744 | tf_op jit(solution)/shard_map/ppermute | solution.py:276
  189.3 23.2 %collective-permute-start.27 = (bf16[288,512]{1,0:T(8,128)(2,1)}, bf16[288,512]{1,0:T(8,128)(2,1)}, u32[]{:S(2)}, u32[]{:S(2)}) collective-permute-start(bf16[288,512]{1,0:T(8,128)(2,1)} %get-tuple-element.71), channel_id=1, source_target_pairs={{0,48},{16,0},{32,16},{48,32},{64,112},{80,64},{96,80},{112,96},{1... | collective-permute-start | bytes 884744 | tf_op jit(solution)/shard_map/ppermute | solution.py:276
  189.3 7.3 %copy-start.5 = (bf16[2048,128]{1,0:T(8,128)(2,1)}, bf16[2048,128]{1,0:T(8,128)(2,1)S(1)}, u32[]{:S(2)}) copy-start(bf16[2048,128]{1,0:T(8,128)(2,1)S(1)} %collective-permute-done.30.refs_0_) | copy-start | bytes 1572868
  189.3 27.8 %collective-permute-start.26 = (bf16[288,512]{1,0:T(8,128)(2,1)}, bf16[288,512]{1,0:T(8,128)(2,1)}, u32[]{:S(2)}, u32[]{:S(2)}) collective-permute-start(bf16[288,512]{1,0:T(8,128)(2,1)} %get-tuple-element.70), channel_id=1, source_target_pairs={{0,16},{16,32},{32,48},{48,0},{64,80},{80,96},{96,112},{112,64},{1... | collective-permute-start | bytes 884744 | tf_op jit(solution)/shard_map/ppermute | solution.py:276
  191.3 25.8 %collective-permute-start.25 = (bf16[288,512]{1,0:T(8,128)(2,1)}, bf16[288,512]{1,0:T(8,128)(2,1)}, u32[]{:S(2)}, u32[]{:S(2)}) collective-permute-start(bf16[288,512]{1,0:T(8,128)(2,1)} %get-tuple-element.69), channel_id=1, source_target_pairs={{0,112},{16,64},{32,80},{48,96},{64,48},{80,0},{96,16},{112,32},{1... | collective-permute-start | bytes 884744 | tf_op jit(solution)/shard_map/ppermute | solution.py:276
  193.8 0.8 copy-start.6
  194.6 24.8 %collective-permute-start.24 = (bf16[288,512]{1,0:T(8,128)(2,1)}, bf16[288,512]{1,0:T(8,128)(2,1)}, u32[]{:S(2)}, u32[]{:S(2)}) collective-permute-start(bf16[288,512]{1,0:T(8,128)(2,1)} %get-tuple-element.68), channel_id=1, source_target_pairs={{0,80},{16,96},{32,112},{48,64},{64,16},{80,32},{96,48},{112,0},{1... | collective-permute-start | bytes 884744 | tf_op jit(solution)/shard_map/ppermute | solution.py:276
  207.2 47.1 %copy-start.8 = (bf16[288,512]{1,0:T(8,128)(2,1)S(1)}, bf16[288,512]{1,0:T(8,128)(2,1)}, u32[]{:S(2)}) copy-start(bf16[288,512]{1,0:T(8,128)(2,1)} %get-tuple-element.99) | copy-start | bytes 884740
  207.2 18.2 %collective-permute-start.23 = (bf16[288,512]{1,0:T(8,128)(2,1)}, bf16[288,512]{1,0:T(8,128)(2,1)S(1)}, u32[]{:S(2)}, u32[]{:S(2)}) collective-permute-start(bf16[288,512]{1,0:T(8,128)(2,1)} %get-tuple-element.67), channel_id=1, source_target_pairs={{0,32},{16,48},{32,0},{48,16},{64,96},{80,112},{96,64},{112,80},{1... | collective-permute-start | bytes 884744 | tf_op jit(solution)/shard_map/ppermute | solution.py:276
  212.5 16.0 %collective-permute-start.22 = (bf16[288,512]{1,0:T(8,128)(2,1)}, bf16[288,512]{1,0:T(8,128)(2,1)S(1)}, u32[]{:S(2)}, u32[]{:S(2)}) collective-permute-start(bf16[288,512]{1,0:T(8,128)(2,1)} %get-tuple-element.66), channel_id=1, source_target_pairs={{0,96},{16,112},{32,64},{48,80},{64,32},{80,48},{96,0},{112,16},{1... | collective-permute-start | bytes 884744 | tf_op jit(solution)/shard_map/ppermute | solution.py:276
  217.1 14.0 %collective-permute-start.39 = (bf16[288,512]{1,0:T(8,128)(2,1)}, bf16[288,512]{1,0:T(8,128)(2,1)}, u32[]{:S(2)}, u32[]{:S(2)}) collective-permute-start(bf16[288,512]{1,0:T(8,128)(2,1)} %get-tuple-element.90), channel_id=1, source_target_pairs={{0,64},{16,80},{32,96},{48,112},{64,0},{80,16},{96,32},{112,48},{1... | collective-permute-start | bytes 884744 | tf_op jit(solution)/shard_map/ppermute | solution.py:276
  217.1 23.4 %collective-permute-start.38 = (bf16[288,512]{1,0:T(8,128)(2,1)}, bf16[288,512]{1,0:T(8,128)(2,1)}, u32[]{:S(2)}, u32[]{:S(2)}) collective-permute-start(bf16[288,512]{1,0:T(8,128)(2,1)} %get-tuple-element.89), channel_id=1, source_target_pairs={{0,48},{16,0},{32,16},{48,32},{64,112},{80,64},{96,80},{112,96},{1... | collective-permute-start | bytes 884744 | tf_op jit(solution)/shard_map/ppermute | solution.py:276
  219.4 23.4 %collective-permute-start.37 = (bf16[288,512]{1,0:T(8,128)(2,1)}, bf16[288,512]{1,0:T(8,128)(2,1)}, u32[]{:S(2)}, u32[]{:S(2)}) collective-permute-start(bf16[288,512]{1,0:T(8,128)(2,1)} %get-tuple-element.88), channel_id=1, source_target_pairs={{0,16},{16,32},{32,48},{48,0},{64,80},{80,96},{96,112},{112,64},{1... | collective-permute-start | bytes 884744 | tf_op jit(solution)/shard_map/ppermute | solution.py:276
  225.4 17.4 %collective-permute-start.36 = (bf16[288,512]{1,0:T(8,128)(2,1)}, bf16[288,512]{1,0:T(8,128)(2,1)}, u32[]{:S(2)}, u32[]{:S(2)}) collective-permute-start(bf16[288,512]{1,0:T(8,128)(2,1)} %get-tuple-element.87), channel_id=1, source_target_pairs={{0,112},{16,64},{32,80},{48,96},{64,48},{80,0},{96,16},{112,32},{1... | collective-permute-start | bytes 884744 | tf_op jit(solution)/shard_map/ppermute | solution.py:276
  228.4 15.7 %collective-permute-start.35 = (bf16[288,512]{1,0:T(8,128)(2,1)}, bf16[288,512]{1,0:T(8,128)(2,1)}, u32[]{:S(2)}, u32[]{:S(2)}) collective-permute-start(bf16[288,512]{1,0:T(8,128)(2,1)} %get-tuple-element.86), channel_id=1, source_target_pairs={{0,80},{16,96},{32,112},{48,64},{64,16},{80,32},{96,48},{112,0},{1... | collective-permute-start | bytes 884744 | tf_op jit(solution)/shard_map/ppermute | solution.py:276
  231.2 20.2 %collective-permute-start.34 = (bf16[288,512]{1,0:T(8,128)(2,1)}, bf16[288,512]{1,0:T(8,128)(2,1)}, u32[]{:S(2)}, u32[]{:S(2)}) collective-permute-start(bf16[288,512]{1,0:T(8,128)(2,1)} %get-tuple-element.85), channel_id=1, source_target_pairs={{0,32},{16,48},{32,0},{48,16},{64,96},{80,112},{96,64},{112,80},{1... | collective-permute-start | bytes 884744 | tf_op jit(solution)/shard_map/ppermute | solution.py:276
  240.5 10.9 %collective-permute-start.33 = (bf16[288,512]{1,0:T(8,128)(2,1)}, bf16[288,512]{1,0:T(8,128)(2,1)}, u32[]{:S(2)}, u32[]{:S(2)}) collective-permute-start(bf16[288,512]{1,0:T(8,128)(2,1)} %get-tuple-element.84), channel_id=1, source_target_pairs={{0,96},{16,112},{32,64},{48,80},{64,32},{80,48},{96,0},{112,16},{1... | collective-permute-start | bytes 884744 | tf_op jit(solution)/shard_map/ppermute | solution.py:276
  242.9 14.1 %collective-permute-start.29 = (f32[144,512]{1,0:T(8,128)}, f32[144,512]{1,0:T(8,128)}, u32[]{:S(2)}, u32[]{:S(2)}) collective-permute-start(f32[144,512]{1,0:T(8,128)} %convert_add_fusion.3), channel_id=1, source_target_pairs={{0,8},{8,0},{1,9},{9,1},{2,10},{10,2},{3,11},{11,3},{4,12},{12,4},... | collective-permute-start | bytes 884744 | tf_op jit(solution)/shard_map/ppermute | solution.py:282
  253.7 3.3 %collective-permute-start.40 = (f32[144,512]{1,0:T(8,128)}, f32[144,512]{1,0:T(8,128)}, u32[]{:S(2)}, u32[]{:S(2)}) collective-permute-start(f32[144,512]{1,0:T(8,128)} %convert_add_fusion.1), channel_id=1, source_target_pairs={{0,8},{8,0},{1,9},{9,1},{2,10},{10,2},{3,11},{11,3},{4,12},{12,4},... | collective-permute-start | bytes 884744 | tf_op jit(solution)/shard_map/ppermute | solution.py:282
  (2 other events, 1.4 us)
where the time goes:
time: 262 us; the launch traced here: 260 us
  starting transfers between devices  74.2 us (28%)
  waiting for transfers between devices  70.6 us (27%)
  Pallas kernels  39.1 us (15%)
  blocking collectives  38.7 us (15%)
  other arithmetic  15.9 us (6%)
  local copies, waits for them, and re-layouts  13.7 us (5%)
  matrix products  4.15 us (2%)
  between operations  3.72 us (1%)
    ppermute x14, starting transfers between devices, step(): sums.append(lax.ppermute(part, ZY, shift_zy(i)) if i else part)  35.7 us
    ppermute x7, waiting for transfers between devices, step(): lax.ppermute(window, ZY, shift_zy(i))  24.8 us
    ppermute x14, waiting for transfers between devices, step(): sums.append(lax.ppermute(part, ZY, shift_zy(i)) if i else part)  22.4 us
    pallas_call x2, Pallas kernels, partial_rows(): pl.pallas_call(partial_kernel, out_shape=[jax.ShapeDtypeStruct((rows, 4 *...  21.3 us
    all_to_all x1, blocking collectives, step(): kept = lax.all_to_all(kept.reshape(8, -1, n_half), ZY, 0, 0)  19.5 us
    all_to_all x1, blocking collectives, spread(): lax.all_to_all(jnp.broadcast_to(x[None], (count,) + x.shape), axes, 0, 0)  19.2 us
    pallas_call x1, Pallas kernels, moved_blocks(): pl.pallas_call(moved_kernel, out_shape=jax.ShapeDtypeStruct((CHIP * TILE,...  14.7 us
    all_to_all x2, starting transfers between devices, spread(): lax.all_to_all(jnp.broadcast_to(x[None], (count,) + x.shape), axes, 0, 0)  12.4 us
  transfers between devices with their start and end apart: 44, of which 15 were waited for; matrix products, arithmetic and copies ran while one was open for 5% of the time, Pallas kernels for 14%

commit v1 on v0

--- a/solution.py
+++ b/solution.py
@@ -51,31 +51,32 @@
         at = pl.multiple_of(g * 128, 128)
         occ = tiles_ref[:, 0, :, pl.ds(at, 128)].reshape(128, 128)
         vir = tiles_ref[:, 1, :, pl.ds(at, 128)].reshape(128, 128)
-        oe_ref[...] = jnp.dot(occ, eo_ref[...], preferred_element_type=F32)
-        ve_ref[...] = jnp.dot(vir, ev_ref[...], preferred_element_type=F32)
+        numbers = (((0,), (0,)), ((), ()))
+        oe_ref[...] = lax.dot_general(occ, eo_ref[...], numbers, preferred_element_type=F32)
+        ve_ref[...] = lax.dot_general(vir, ev_ref[...], numbers, preferred_element_type=F32)
         for r in range(8):
-            win_ref[r] = all_ref[where_ref[g * 8 + r]].T
+            win_ref[r] = all_ref[where_ref[g * 8 + r]]
 
         def target(s, c):
-            rows = pl.multiple_of(s * BS, BS)
-            to = pl.multiple_of(s * TILE, TILE)
-            total = acc_ref[pl.ds(to, TILE), :]
+            at = pl.multiple_of(s * TILE, TILE)
+            total = acc_ref[s]
             for r in range(8):
-                v = ve_ref[pl.ds(rows, BS), r * TILE:(r + 1) * TILE]
+                v = ve_ref[r * BS:(r + 1) * BS, pl.ds(at, TILE)]
                 kron = jnp.concatenate(
                     [
-                        (oe_ref[pl.ds(rows + i, 1), r * TILE:(r + 1) * TILE] * v).astype(BF16)
-                        for i in range(BS)
+                        (oe_ref[r * BS + j:r * BS + j + 1, pl.ds(at, TILE)] * v).astype(BF16)
+                        for j in range(BS)
                     ], axis=0)
-                total = total + jnp.dot(kron, win_ref[r], preferred_element_type=F32)
-            acc_ref[pl.ds(to, TILE), :] = total
+                total = total + jnp.dot(win_ref[r], kron, preferred_element_type=F32)
+            acc_ref[s] = total
             return c
 
-        carry = lax.fori_loop(0, bound_ref[0], target, carry)
-        return lax.fori_loop(OWN, OWN + bound_ref[1], target, carry)
+        return lax.fori_loop(0, CHIP, target, carry, unroll=4)
 
     lax.fori_loop(0, LIVE // 8, group, 0)
-    out_ref[...] = acc_ref[...].astype(BF16)
+    for s in range(CHIP):
+        live = s % OWN < bound_ref[s // OWN]
+        out_ref[s * TILE:(s + 1) * TILE] = jnp.where(live, acc_ref[s].T, 0.0).astype(BF16)
 
 
 def moved_blocks(where, bounds, tiles, pieces):
@@ -87,12 +88,12 @@
         in_specs=[sm, sm, vm] + [pl.BlockSpec(memory_space=pl.ANY)] * 16,
         out_specs=vm,
         scratch_shapes=[
-            pltpu.VMEM((CHIP * TILE, WIN_DEV), F32),
+            pltpu.VMEM((CHIP, WIN_DEV, TILE), F32),
             pltpu.VMEM((128, 2048), BF16),
             pltpu.VMEM((128, 2048), BF16),
             pltpu.VMEM((128, 2048), F32),
             pltpu.VMEM((128, 2048), F32),
-            pltpu.VMEM((8, TILE, WIN_DEV), BF16),
+            pltpu.VMEM((8, WIN_DEV, TILE), BF16),
             pltpu.VMEM((16 * OWN, WIN_DEV, TILE), BF16),
             pltpu.SemaphoreType.DMA((16,)),
         ],
@@ -172,10 +173,6 @@
     aux_rows = three_center.shape[0]
     chip_rows = aux_rows // 8
 
-    window = jnp.transpose(three_center[:WIN_DEV], (1, 0, 2))
-    near = [window] + [lax.ppermute(window, ZY, shift_zy(i)) for i in range(1, 8)]
-    windows = near + [lax.ppermute(piece, "c", SWAP) for piece in near]
-
     facts = jnp.concatenate([pair_blocks.reshape(-1), block_count])
     facts = jnp.pad(facts, (0, 128 - facts.shape[0]))
     facts = jnp.broadcast_to(facts[None], (8, 128))
@@ -215,16 +212,28 @@
     base_own = lax.dynamic_index_in_dim(before, group, 0, keepdims=False)
     base_next = lax.dynamic_index_in_dim(before, group + 1 - 2 * c, 0, keepdims=False)
     given = lax.ppermute(given, "c", SWAP)
-    given, base_own, base_next = lax.optimization_barrier((given, base_own, base_next))
+    yo = 1 - yl
+    xp, xm, x2 = (x - 1) % 4, (x + 1) % 4, (x + 2) % 4
+    place = jnp.stack([yl * 4 + x, yo * 4 + x, yl * 4 + xp, yl * 4 + xm,
+                       yo * 4 + xp, yo * 4 + xm, yl * 4 + x2, yo * 4 + x2]).astype(jnp.int32)
+    order = (6, 2, 5, 7, 1, 3, 4, 0)
+    dests = jnp.stack([((y + i // 4) % 2) * 4 + (z + i % 4) % 4 for i in order]).astype(jnp.int32)
+    given, base_own, base_next, place, dests = lax.optimization_barrier(
+        (given, base_own, base_next, place, dests))
     kept = kept + given
     kept = lax.all_to_all(kept.reshape(8, -1, n_half), ZY, 0, 0)
+    mine = three_center.reshape(aux_rows, OWN * TILE)
+    window = jnp.transpose(three_center[:WIN_DEV], (1, 0, 2))
+    tau = jnp.sum(jnp.where(jnp.arange(2) == c, tau_points, 0.0), keepdims=True)
+    kept, mine, window, tau = lax.optimization_barrier((kept, mine, window, tau))
+    near = [window] + [lax.ppermute(window, ZY, shift_zy(i)) for i in range(1, 8)]
+    windows = near + [lax.ppermute(piece, "c", SWAP) for piece in near]
     kept = jnp.sum(kept.astype(F32), axis=0).astype(BF16)
     kept = spread(kept, ZY, 8).reshape(LIVE * BS, n_half)
     given = lax.ppermute(kept, "c", SWAP)
     rows = jnp.concatenate(
         [jnp.where(c == 0, kept, given), jnp.where(c == 0, given, kept)], axis=1)
 
-    tau = jnp.where(c == 0, tau_points[0], tau_points[1])
     factor = jnp.concatenate([jnp.exp(tau * e_occ / 2.0), jnp.exp(-tau * e_vir / 2.0)])
     scaled = (rows.astype(F32) * factor[None, :]).astype(BF16)
     padded = jnp.concatenate([scaled, jnp.zeros((OWN * BS, scaled.shape[1]), BF16)], axis=0)
@@ -240,11 +249,10 @@
             lax.dot_general(own[:, n_occ:], scaled[:, n_occ:], numbers, preferred_element_type=F32),
         ])
     grams = grams.reshape(2, CHIP, BS, LIVE * BS).transpose(1, 0, 2, 3)
-    grams, three_center = lax.optimization_barrier((grams, three_center))
-    mine = three_center.reshape(aux_rows, OWN * TILE)
-    other = lax.ppermute(mine, "c", SWAP)
     grams = jnp.sum(lax.all_to_all(grams, AUX, 0, 0), axis=0)
     grams = grams.astype(BF16)
+    grams, mine = lax.optimization_barrier((grams, mine))
+    other = lax.ppermute(mine, "c", SWAP)
     tiles = spread(grams, AUX, 8)
 
     bounds = jnp.stack([
@@ -258,27 +266,27 @@
     byp = lax.ppermute(by, "x", XP)
     bym = lax.ppermute(by, "x", XM)
     bpp = lax.ppermute(bp, "x", XP)
-    order = (6, 2, 5, 7, 1, 3, 4, 0)
-    dests = jnp.stack([((y + i // 4) % 2) * 4 + (z + i % 4) % 4 for i in order]).astype(jnp.int32)
     partials = [partial_rows(dests, mine, other, [moved, by, bp, bm])]
     bym, partials[0] = lax.optimization_barrier((bym, partials[0]))
     bymm = lax.ppermute(bym, "x", XM)
     partials.append(partial_rows(dests, mine, other, [byp, bym, bpp, bymm]))
-    yo = 1 - yl
-    xp, xm, x2 = (x - 1) % 4, (x + 1) % 4, (x + 2) % 4
-    place = jnp.stack([yl * 4 + x, yo * 4 + x, yl * 4 + xp, yl * 4 + xm,
-                       yo * 4 + xp, yo * 4 + xm, yl * 4 + x2, yo * 4 + x2]).astype(jnp.int32)
     rows_dev = chip_rows // 2
     ends = []
     for partial in partials:
         sums = []
         for i, part in zip(order, partial):
             sums.append(lax.ppermute(part, ZY, shift_zy(i)) if i else part)
-        leave = sum(lax.dynamic_slice_in_dim(part, (1 - c) * rows_dev, rows_dev, 0).astype(F32)
-                    for part in sums)
-        leave, *sums = lax.optimization_barrier((leave, *sums))
-        stay = sum(lax.dynamic_slice_in_dim(part, c * rows_dev, rows_dev, 0).astype(F32)
-                   for part in sums)
+
+        def half_of(which, picked):
+            return sum(
+                lax.dynamic_slice_in_dim(part, which * rows_dev, rows_dev, 0).astype(F32)
+                for i, part in zip(order, sums) if picked(i))
+
+        leave, stay = lax.optimization_barrier(
+            (half_of(1 - c, lambda i: i < 4), half_of(c, lambda i: i < 4)))
+        leave = leave + half_of(1 - c, lambda i: i >= 4)
+        leave, stay, *sums = lax.optimization_barrier((leave, stay, *sums))
+        stay = stay + half_of(c, lambda i: i >= 4)
         ends += [stay, lax.ppermute(leave, "c", SWAP)]
     return finish(c.astype(jnp.int32).reshape(1), place, ends)
 

time: 262 us -> 263 us (level)
  waiting for transfers between devices: 70.6 us -> 79.5 us
  starting transfers between devices: 74.2 us -> 66.6 us
  local copies, waits for them, and re-layouts: 13.7 us -> 16.8 us
    all_to_all x1, waiting for transfers between devices: 0.01 us -> 7.51 us  [step(): kept = lax.all_to_all(kept.reshape(8, -1, n_half), ZY, 0, 0)]
    ppermute x14, waiting for transfers between devices: 22.4 us -> 28.5 us  [step(): sums.append(lax.ppermute(part, ZY, shift_zy(i)) if i else part)]
    ppermute x14, starting transfers between devices: 35.7 us -> 29.6 us  [step(): sums.append(lax.ppermute(part, ZY, shift_zy(i)) if i else part)]
    ppermute x7, waiting for transfers between devices: 24.8 us -> 21.3 us  [step(): lax.ppermute(window, ZY, shift_zy(i))]
    all_to_all x1, blocking collectives: 19.5 us -> 16.2 us  [step(): grams = jnp.sum(lax.all_to_all(grams, AUX, 0, 0), axis=0)]
    unnamed x47 -> x45, local copies, waits for them, and re-layouts: 7.81 us -> 10.6 us
    add x3 -> x5, other arithmetic: 6.92 us -> 5.76 us  [the longest x2 2.75 us: half_of(): sum((lax.dynamic_slice_in_dim(part, which * rows_dev, rows_dev, 0).astype...]
  transfers between devices with their start and end apart: 44 -> 44, of which waited for: 15 -> 17; matrix products, arithmetic and copies ran while one was open for 5% -> 8% of each run, Pallas kernels for 14% -> 14%
where the time goes in v1:
time: 263 us; the launch traced here: 260 us
  waiting for transfers between devices  79.5 us (30%)
  starting transfers between devices  66.6 us (25%)
  Pallas kernels  38.5 us (15%)
  blocking collectives  37.2 us (14%)
  local copies, waits for them, and re-layouts  16.8 us (6%)
  other arithmetic  15.7 us (6%)
  matrix products  3.11 us (1%)
  between operations  2.99 us (1%)
    ppermute x14, starting transfers between devices, step(): sums.append(lax.ppermute(part, ZY, shift_zy(i)) if i else part)  29.6 us
    ppermute x14, waiting for transfers between devices, step(): sums.append(lax.ppermute(part, ZY, shift_zy(i)) if i else part)  28.5 us
    pallas_call x2, Pallas kernels, partial_rows(): pl.pallas_call(partial_kernel, out_shape=[jax.ShapeDtypeStruct((rows, 4 *...  21.3 us
    ppermute x7, waiting for transfers between devices, step(): lax.ppermute(window, ZY, shift_zy(i))  21.3 us
    all_to_all x1, blocking collectives, spread(): lax.all_to_all(jnp.broadcast_to(x[None], (count,) + x.shape), axes, 0, 0)  21 us
    all_to_all x1, blocking collectives, step(): grams = jnp.sum(lax.all_to_all(grams, AUX, 0, 0), axis=0)  16.2 us
    pallas_call x1, Pallas kernels, moved_blocks(): pl.pallas_call(moved_kernel, out_shape=jax.ShapeDtypeStruct((CHIP * TILE,...  14.1 us
    all_to_all x2, starting transfers between devices, spread(): lax.all_to_all(jnp.broadcast_to(x[None], (count,) + x.shape), axes, 0, 0)  11.6 us
  transfers between devices with their start and end apart: 44, of which 17 were waited for; matrix products, arithmetic and copies ran while one was open for 8% of the time, Pallas kernels for 14%

profile of v1, /device:TPU:0, one launch (start us, length us, event | category | flops | bytes accessed | tf_op | source)
XLA Modules:
  0.0 260.3 jit_solution(7349526292947832592)
XLA Ops:
  0.0 0.9 copy.23
  1.7 0.6 broadcast_in_dim_broadcast_in_dim_broadcast_in_dim.2
  2.4 8.2 %all-to-all-start = ((s32[16,8,128]{2,1,0:T(8,128)}), s32[16,8,128]{2,1,0:T(8,128)S(1)}, u32[]{:S(2)}, u32[]{:S(2)}) async-start(s32[16,8,128]{2,1,0:T(8,128)} %broadcast_in_dim_broadcast_in_dim_broadcast_in_dim.2), calls=%async_computation | async-start | bytes 131072 | tf_op jit(solution)/shard_map/all_to_all | solution.py:29
  10.7 7.6 %all-to-all-done = s32[16,8,128]{2,1,0:T(8,128)S(1)} async-done(((s32[16,8,128]{2,1,0:T(8,128)}), s32[16,8,128]{2,1,0:T(8,128)S(1)}, u32[]{:S(2)}, u32[]{:S(2)}) %all-to-all-start) | async-done | bytes 65568 | tf_op jit(solution)/shard_map/all_to_all | solution.py:29
  19.4 1.7 convolution_convert_fusion
  21.7 1.2 broadcast_select_fusion.2
  22.9 0.7 stack.85.dest_ref
  24.2 0.7 fusion.24
  24.9 0.8 collective-permute-done
  25.6 2.8 %select_add_fusion = bf16[640,768]{1,0:T(8,128)(2,1)} fusion(bf16[640,768]{1,0:T(8,128)(2,1)S(1)} %collective-permute-done, pred[]{:T(512)S(6)} %eq.95, bf16[640,1408]{1,0:T(8,128)(2,1)} %copy-done.1, bf16[640,128]{1,0:T(8,128)(2,1)S(1)} %fusion.3), kind=kLoop, calls=%fused_computation.11 | loop fusion | flops 4423680 | bytes 4915201 | tf_op jit(solution)/shard_map/add | solution.py:223
  28.4 3.6 %all-to-all-start.1 = ((bf16[8,80,768]{2,1,0:T(8,128)(2,1)}), bf16[8,80,768]{2,1,0:T(8,128)(2,1)S(1)}, u32[]{:S(2)}, u32[]{:S(2)}) async-start(bf16[8,80,768]{2,1,0:T(8,128)(2,1)} %bitcast.22), calls=%async_computation.1 | async-start | bytes 1966080 | tf_op jit(solution)/shard_map/all_to_all | solution.py:224
  32.0 1.0 slice.45
  33.0 6.0 %copy.31 = bf16[288,8,4,256]{3,1,2,0:T(8,128)(2,1)} copy(bf16[288,8,4,256]{3,2,1,0:T(4,128)(2,1)} %bitcast.50) | data formatting | bytes 9437184
  39.7 7.5 %all-to-all-done.1 = bf16[8,80,768]{2,1,0:T(8,128)(2,1)S(1)} async-done(((bf16[8,80,768]{2,1,0:T(8,128)(2,1)}), bf16[8,80,768]{2,1,0:T(8,128)(2,1)S(1)}, u32[]{:S(2)}, u32[]{:S(2)}) %all-to-all-start.1) | async-done | bytes 983072 | tf_op jit(solution)/shard_map/all_to_all | solution.py:224
  47.4 21.0 %all_to_all.25 = bf16[8,80,768]{2,1,0:T(8,128)(2,1)S(1)} all-to-all(bf16[8,80,768]{2,1,0:T(8,128)(2,1)S(1)} %broadcast_in_dim.108), channel_id=1, replica_groups=mesh['yh'=2,'z'=4,'c'=2,'yl'=2,'x'=4] {'yh','z'}, dimensions={0} | all-to-all | bytes 1966080 | tf_op jit(solution)/shard_map/all_to_all | solution.py:29
  71.1 1.3 broadcast_select_fusion.1
  73.1 0.7 fusion.1
  73.8 16.2 %all_to_all.26 = f32[8,2,16,640]{3,2,1,0:T(8,128)S(1)} all-to-all(f32[8,2,16,640]{3,2,1,0:T(8,128)S(1)} %maximum_bitcast_fusion), channel_id=1, replica_groups=mesh['yh'=2,'z'=4,'c'=2,'yl'=2,'x'=4] {'yl','x'}, dimensions={0} | all-to-all | bytes 1310720 | tf_op jit(solution)/shard_map/all_to_all | solution.py:252
  90.6 2.1 collective-permute-start.3
  92.6 1.1 collective-permute-start.4
  93.7 1.5 collective-permute-start.5
  95.2 10.4 %collective-permute-done.2.refs_1_ = bf16[4,128,256]{2,1,0:T(8,128)(2,1)S(1)} collective-permute-done((bf16[4,128,256]{2,1,0:T(8,128)(2,1)S(1)}, bf16[4,128,256]{2,1,0:T(8,128)(2,1)S(1)}, u32[]{:S(2)}, u32[]{:S(2)}) %collective-permute-start.2) | collective-permute-done | bytes 262176 | tf_op jit(solution)/shard_map/ppermute | solution.py:229
  105.8 3.0 %collective-permute-start.7 = (bf16[4,128,256]{2,1,0:T(8,128)(2,1)S(1)}, bf16[4,128,256]{2,1,0:T(8,128)(2,1)S(1)}, u32[]{:S(2)}, u32[]{:S(2)}) collective-permute-start(bf16[4,128,256]{2,1,0:T(8,128)(2,1)S(1)} %bitcast.58), channel_id=1, source_target_pairs={{0,96},{16,112},{32,64},{48,80},{64,32},{80,48},{96,0},{112,16},{1... | collective-permute-start | bytes 786440 | tf_op jit(solution)/shard_map/ppermute | solution.py:229
  108.9 2.4 collective-permute-start.8
  111.4 9.2 %collective-permute-done.6.refs_5_ = bf16[4,128,256]{2,1,0:T(8,128)(2,1)S(1)} collective-permute-done((bf16[4,128,256]{2,1,0:T(8,128)(2,1)S(1)}, bf16[4,128,256]{2,1,0:T(8,128)(2,1)S(1)}, u32[]{:S(2)}, u32[]{:S(2)}) %collective-permute-start.6) | collective-permute-done | bytes 262176 | tf_op jit(solution)/shard_map/ppermute | solution.py:229
  120.6 1.4 collective-permute-done.7.refs_6_
  122.1 0.7 copy-done.12
  122.7 0.7 copy-done.13
  123.4 0.8 broadcast_in_dim.109
  124.1 3.4 %all-to-all-start.4 = ((bf16[8,2,16,640]{3,2,1,0:T(8,128)(2,1)}), bf16[8,2,16,640]{3,2,1,0:T(8,128)(2,1)S(1)}, u32[]{:S(2)}, u32[]{:S(2)}) async-start(bf16[8,2,16,640]{3,2,1,0:T(8,128)(2,1)} %broadcast_in_dim.109), calls=%async_computation.4 | async-start | bytes 655360 | tf_op jit(solution)/shard_map/all_to_all | solution.py:29
  129.6 1.9 pad_add_fusion.1.bound_ref
  131.5 0.7 select_reduce_fusion.1.where_ref
  132.2 0.7 copy-done.16
  133.0 3.5 %all-to-all-done.4.tiles_ref = bf16[8,2,16,640]{3,2,1,0:T(8,128)(2,1)S(1)} async-done(((bf16[8,2,16,640]{3,2,1,0:T(8,128)(2,1)}), bf16[8,2,16,640]{3,2,1,0:T(8,128)(2,1)S(1)}, u32[]{:S(2)}, u32[]{:S(2)}) %all-to-all-start.4) | async-done | bytes 327712 | tf_op jit(solution)/shard_map/all_to_all | solution.py:29
  136.5 0.7 copy-done.2
  137.2 14.1 %moved.1.refs_0_ = bf16[2048,128]{1,0:T(8,128)(2,1)} custom-call(s32[40]{0:T(128)} %select_reduce_fusion.1.where_ref, s32[2]{0:T(128)} %pad_add_fusion.1.bound_ref, bf16[8,2,16,640]{3,2,1,0:T(8,128)(2,1)} %copy-done.2, bf16[4,128,256]{2,1,0:T(8,128)(2,1)} %bitcast.61, bf16[4,128,256]{2,1,0:T(8,128)(2,1)} %copy-done.8, bf16[4,128,256]{2,1,0:T(8,128)(2,1)} %copy-done.9, ...), custom_call_target="tpu_custom_call" | custom-call | tf_op jit(solution)/shard_map/moved/pallas_call | solution.py:85
  151.9 0.9 collective-permute-start.20
  152.8 2.4 collective-permute-start.21
  155.2 10.1 %collective-permute-done.17.refs_1_ = bf16[2048,128]{1,0:T(8,128)(2,1)} collective-permute-done((bf16[2048,128]{1,0:T(8,128)(2,1)}, bf16[2048,128]{1,0:T(8,128)(2,1)}, u32[]{:S(2)}, u32[]{:S(2)}) %collective-permute-start.17) | collective-permute-done | bytes 524320 | tf_op jit(solution)/shard_map/ppermute | solution.py:263
  165.5 1.8 collective-permute-start.30
  167.8 10.7 %partial.2 = (bf16[288,512]{1,0:T(8,128)(2,1)}, bf16[288,512]{1,0:T(8,128)(2,1)}, bf16[288,512]{1,0:T(8,128)(2,1)}, bf16[288,512]{1,0:T(8,128)(2,1)}, bf16[288,5...) custom-call(s32[8]{0:T(128)} %stack.85.dest_ref, ...), custom_call_target="tpu_custom_call" | custom-call | tf_op jit(solution)/shard_map/partial/pallas_call | solution.py:131
  178.5 3.1 %collective-permute-start.32 = (bf16[2048,128]{1,0:T(8,128)(2,1)S(1)}, bf16[2048,128]{1,0:T(8,128)(2,1)S(1)}, u32[]{:S(2)}, u32[]{:S(2)}) collective-permute-start(bf16[2048,128]{1,0:T(8,128)(2,1)S(1)} %collective-permute-done.18.refs_1_), channel_id=1, source_target_pairs={{0,3},{1,0},{2,1},{3,2},{4,7},{5,4},{6,5},{7,6},{8,11},{9,8},{10,9... | collective-permute-start | bytes 1572872 | tf_op jit(solution)/shard_map/ppermute | solution.py:271
  181.6 7.7 %collective-permute-start.22 = (bf16[288,512]{1,0:T(8,128)(2,1)}, bf16[288,512]{1,0:T(8,128)(2,1)}, u32[]{:S(2)}, u32[]{:S(2)}) collective-permute-start(bf16[288,512]{1,0:T(8,128)(2,1)} %get-tuple-element.76), channel_id=1, source_target_pairs={{0,32},{16,48},{32,0},{48,16},{64,96},{80,112},{96,64},{112,80},{1... | collective-permute-start | bytes 884744 | tf_op jit(solution)/shard_map/ppermute | solution.py:278
  189.4 3.2 %collective-permute-start.24 = (bf16[288,512]{1,0:T(8,128)(2,1)}, bf16[288,512]{1,0:T(8,128)(2,1)}, u32[]{:S(2)}, u32[]{:S(2)}) collective-permute-start(bf16[288,512]{1,0:T(8,128)(2,1)} %get-tuple-element.78), channel_id=1, source_target_pairs={{0,48},{16,0},{32,16},{48,32},{64,112},{80,64},{96,80},{112,96},{1... | collective-permute-start | bytes 884744 | tf_op jit(solution)/shard_map/ppermute | solution.py:278
  192.6 2.1 collective-permute-start.25
  194.7 0.8 copy-done.6
  195.5 1.2 collective-permute-start.26
  196.8 10.7 %partial.3 = (bf16[288,512]{1,0:T(8,128)(2,1)}, bf16[288,512]{1,0:T(8,128)(2,1)}, bf16[288,512]{1,0:T(8,128)(2,1)}, bf16[288,512]{1,0:T(8,128)(2,1)}, bf16[288,5...) custom-call(s32[8]{0:T(128)} %stack.85.dest_ref, ...), custom_call_target="tpu_custom_call" | custom-call | tf_op jit(solution)/shard_map/partial/pallas_call | solution.py:131
  207.4 3.0 %collective-permute-done.22 = bf16[288,512]{1,0:T(8,128)(2,1)} collective-permute-done((bf16[288,512]{1,0:T(8,128)(2,1)}, bf16[288,512]{1,0:T(8,128)(2,1)}, u32[]{:S(2)}, u32[]{:S(2)}) %collective-permute-start.22) | collective-permute-done | bytes 294944 | tf_op jit(solution)/shard_map/ppermute | solution.py:278
  210.5 2.5 collective-permute-start.27
  213.0 0.7 collective-permute-done.23
  213.7 4.9 %collective-permute-start.28 = (bf16[288,512]{1,0:T(8,128)(2,1)}, bf16[288,512]{1,0:T(8,128)(2,1)S(1)}, u32[]{:S(2)}, u32[]{:S(2)}) collective-permute-start(bf16[288,512]{1,0:T(8,128)(2,1)} %get-tuple-element.84), channel_id=1, source_target_pairs={{0,64},{16,80},{32,96},{48,112},{64,0},{80,16},{96,32},{112,48},{1... | collective-permute-start | bytes 884744 | tf_op jit(solution)/shard_map/ppermute | solution.py:278
  218.8 3.1 %collective-permute-start.35 = (bf16[288,512]{1,0:T(8,128)(2,1)}, bf16[288,512]{1,0:T(8,128)(2,1)S(1)}, u32[]{:S(2)}, u32[]{:S(2)}) collective-permute-start(bf16[288,512]{1,0:T(8,128)(2,1)} %get-tuple-element.95), channel_id=1, source_target_pairs={{0,48},{16,0},{32,16},{48,32},{64,112},{80,64},{96,80},{112,96},{1... | collective-permute-start | bytes 884744 | tf_op jit(solution)/shard_map/ppermute | solution.py:278
  222.0 1.5 convert_add_fusion.2
  223.5 4.0 %collective-permute-start.36 = (bf16[288,512]{1,0:T(8,128)(2,1)}, bf16[288,512]{1,0:T(8,128)(2,1)S(1)}, u32[]{:S(2)}, u32[]{:S(2)}) collective-permute-start(bf16[288,512]{1,0:T(8,128)(2,1)} %get-tuple-element.98), channel_id=1, source_target_pairs={{0,96},{16,112},{32,64},{48,80},{64,32},{80,48},{96,0},{112,16},{1... | collective-permute-start | bytes 884744 | tf_op jit(solution)/shard_map/ppermute | solution.py:278
  227.5 5.9 %collective-permute-done.28 = bf16[288,512]{1,0:T(8,128)(2,1)S(1)} collective-permute-done((bf16[288,512]{1,0:T(8,128)(2,1)}, bf16[288,512]{1,0:T(8,128)(2,1)S(1)}, u32[]{:S(2)}, u32[]{:S(2)}) %collective-permute-start.28) | collective-permute-done | bytes 294944 | tf_op jit(solution)/shard_map/ppermute | solution.py:278
  233.9 6.8 %collective-permute-done.33 = bf16[288,512]{1,0:T(8,128)(2,1)} collective-permute-done((bf16[288,512]{1,0:T(8,128)(2,1)}, bf16[288,512]{1,0:T(8,128)(2,1)}, u32[]{:S(2)}, u32[]{:S(2)}) %collective-permute-start.33) | collective-permute-done | bytes 294944 | tf_op jit(solution)/shard_map/ppermute | solution.py:278
  240.8 4.2 %collective-permute-done.34 = bf16[288,512]{1,0:T(8,128)(2,1)} collective-permute-done((bf16[288,512]{1,0:T(8,128)(2,1)}, bf16[288,512]{1,0:T(8,128)(2,1)}, u32[]{:S(2)}, u32[]{:S(2)}) %collective-permute-start.34) | collective-permute-done | bytes 294944 | tf_op jit(solution)/shard_map/ppermute | solution.py:278
  244.9 1.0 add_add_fusion.3
  246.1 1.3 convert_add_fusion
  247.4 3.8 %collective-permute-done.38 = bf16[288,512]{1,0:T(8,128)(2,1)S(1)} collective-permute-done((bf16[288,512]{1,0:T(8,128)(2,1)}, bf16[288,512]{1,0:T(8,128)(2,1)S(1)}, u32[]{:S(2)}, u32[]{:S(2)}) %collective-permute-start.38) | collective-permute-done | bytes 294944 | tf_op jit(solution)/shard_map/ppermute | solution.py:278
  251.1 4.0 %collective-permute-done.39 = bf16[288,512]{1,0:T(8,128)(2,1)S(1)} collective-permute-done((bf16[288,512]{1,0:T(8,128)(2,1)}, bf16[288,512]{1,0:T(8,128)(2,1)S(1)}, u32[]{:S(2)}, u32[]{:S(2)}) %collective-permute-start.39) | collective-permute-done | bytes 294944 | tf_op jit(solution)/shard_map/ppermute | solution.py:278
  255.4 1.9 add_add_fusion
  257.3 3.0 %finish.1 = f32[144,2,1024]{2,1,0:T(2,128)} custom-call(s32[1]{0:T(128)} %bitcast.core_ref, s32[8]{0:T(128)} %stack.76.place_ref, f32[144,512]{1,0:T(8,128)} %get-tuple-element.126.refs_0_, f32[144,512]{1,0:T(8,128)} %collective-permute-done.29.refs_1_, f32[144,512]{1,0:T(8,128)} %get-tuple-element.125.refs_2_, f32[144,512]{1,0:T(8,128)} %collective-permute-done.40.refs_3_), custom_call_target="tpu_custom_call" | custom-call | tf_op jit(solution)/shard_map/finish/pallas_call | solution.py:160
  (129 shorter events, 10.2 us)
Async XLA Ops:
  0.0 19.4 %copy-start = (bf16[768,1408]{1,0:T(8,128)(2,1)S(1)}, bf16[768,1408]{1,0:T(8,128)(2,1)}, u32[]{:S(2)}) copy-start(bf16[768,1408]{1,0:T(8,128)(2,1)} %param.9) | copy-start | bytes 6488068
  2.4 15.8 %all-to-all-start = ((s32[16,8,128]{2,1,0:T(8,128)}), s32[16,8,128]{2,1,0:T(8,128)S(1)}, u32[]{:S(2)}, u32[]{:S(2)}) async-start(s32[16,8,128]{2,1,0:T(8,128)} %broadcast_in_dim_broadcast_in_dim_broadcast_in_dim.2), calls=%async_computation | async-start | bytes 131072 | tf_op jit(solution)/shard_map/all_to_all | solution.py:29
  19.4 1.8 copy-start.18
  21.1 1.7 copy-start.1
  22.9 2.8 %collective-permute-start = (bf16[640,768]{1,0:T(8,128)(2,1)}, bf16[640,768]{1,0:T(8,128)(2,1)S(1)}, u32[]{:S(2)}, u32[]{:S(2)}) collective-permute-start(bf16[640,768]{1,0:T(8,128)(2,1)} %broadcast_select_fusion.2), channel_id=1, source_target_pairs={{0,8},{8,0},{1,9},{9,1},{2,10},{10,2},{3,11},{11,3},{4,12},{12,4},... | collective-permute-start | bytes 2949128 | tf_op jit(solution)/shard_map/ppermute | solution.py:214
  28.4 18.8 %all-to-all-start.1 = ((bf16[8,80,768]{2,1,0:T(8,128)(2,1)}), bf16[8,80,768]{2,1,0:T(8,128)(2,1)S(1)}, u32[]{:S(2)}, u32[]{:S(2)}) async-start(bf16[8,80,768]{2,1,0:T(8,128)(2,1)} %bitcast.22), calls=%async_computation.1 | async-start | bytes 1966080 | tf_op jit(solution)/shard_map/all_to_all | solution.py:224
  33.0 6.1 %copy-start.19 = (f32[2]{0:T(128)S(1)}, f32[2]{0:T(128)}, u32[]{:S(2)}) copy-start(f32[2]{0:T(128)} %param.12) | copy-start | bytes 28
  39.1 72.2 %copy-start.3 = (bf16[128,4,256]{2,0,1:T(8,128)(2,1)}, bf16[128,4,256]{2,0,1:T(8,128)(2,1)S(1)}, u32[]{:S(2)}) copy-start(bf16[128,4,256]{2,0,1:T(8,128)(2,1)S(1)} %copy.33) | copy-start | bytes 786436
  47.2 23.0 %copy-start.20 = (f32[128]{0:T(128)S(1)}, f32[128]{0:T(128)}, u32[]{:S(2)}) copy-start(f32[128]{0:T(128)} %param.10) | copy-start | bytes 1540
  47.2 23.6 %copy-start.17 = (f32[1408]{0:T(1024)S(1)}, f32[1408]{0:T(1024)}, u32[]{:S(2)}) copy-start(f32[1408]{0:T(1024)} %param.11) | copy-start | bytes 16900
  68.4 2.7 %collective-permute-start.1 = (bf16[640,768]{1,0:T(8,128)(2,1)S(1)}, bf16[640,768]{1,0:T(8,128)(2,1)}, u32[]{:S(2)}, u32[]{:S(2)}) collective-permute-start(bf16[640,768]{1,0:T(8,128)(2,1)S(1)} %bitcast.51), channel_id=1, source_target_pairs={{0,8},{8,0},{1,9},{9,1},{2,10},{10,2},{3,11},{11,3},{4,12},{12,4},... | collective-permute-start | bytes 2949128 | tf_op jit(solution)/shard_map/ppermute | solution.py:233
  90.1 77.7 %collective-permute-start.19 = (bf16[2304,1024]{1,0:T(8,128)(2,1)}, bf16[2304,1024]{1,0:T(8,128)(2,1)}, u32[]{:S(2)}, u32[]{:S(2)}) collective-permute-start(bf16[2304,1024]{1,0:T(8,128)(2,1)} %bitcast.47), channel_id=1, source_target_pairs={{0,8},{8,0},{1,9},{9,1},{2,10},{10,2},{3,11},{11,3},{4,12},{12,4},... | collective-permute-start | bytes 14155784 | tf_op jit(solution)/shard_map/ppermute | solution.py:255
  90.2 15.4 %collective-permute-start.2 = (bf16[4,128,256]{2,1,0:T(8,128)(2,1)S(1)}, bf16[4,128,256]{2,1,0:T(8,128)(2,1)S(1)}, u32[]{:S(2)}, u32[]{:S(2)}) collective-permute-start(bf16[4,128,256]{2,1,0:T(8,128)(2,1)S(1)} %bitcast.53), channel_id=1, source_target_pairs={{0,16},{16,32},{32,48},{48,0},{64,80},{80,96},{96,112},{112,64},{1... | collective-permute-start | bytes 786440 | tf_op jit(solution)/shard_map/ppermute | solution.py:229
  90.6 15.3 %collective-permute-start.3 = (bf16[4,128,256]{2,1,0:T(8,128)(2,1)S(1)}, bf16[4,128,256]{2,1,0:T(8,128)(2,1)S(1)}, u32[]{:S(2)}, u32[]{:S(2)}) collective-permute-start(bf16[4,128,256]{2,1,0:T(8,128)(2,1)S(1)} %bitcast.54), channel_id=1, source_target_pairs={{0,32},{16,48},{32,0},{48,16},{64,96},{80,112},{96,64},{112,80},{1... | collective-permute-start | bytes 786440 | tf_op jit(solution)/shard_map/ppermute | solution.py:229
  92.6 16.3 %collective-permute-start.4 = (bf16[4,128,256]{2,1,0:T(8,128)(2,1)S(1)}, bf16[4,128,256]{2,1,0:T(8,128)(2,1)}, u32[]{:S(2)}, u32[]{:S(2)}) collective-permute-start(bf16[4,128,256]{2,1,0:T(8,128)(2,1)S(1)} %bitcast.55), channel_id=1, source_target_pairs={{0,48},{16,0},{32,16},{48,32},{64,112},{80,64},{96,80},{112,96},{1... | collective-permute-start | bytes 786440 | tf_op jit(solution)/shard_map/ppermute | solution.py:229
  93.7 17.6 %collective-permute-start.5 = (bf16[4,128,256]{2,1,0:T(8,128)(2,1)S(1)}, bf16[4,128,256]{2,1,0:T(8,128)(2,1)S(1)}, u32[]{:S(2)}, u32[]{:S(2)}) collective-permute-start(bf16[4,128,256]{2,1,0:T(8,128)(2,1)S(1)} %bitcast.56), channel_id=1, source_target_pairs={{0,64},{16,80},{32,96},{48,112},{64,0},{80,16},{96,32},{112,48},{1... | collective-permute-start | bytes 786440 | tf_op jit(solution)/shard_map/ppermute | solution.py:229
  105.6 30.9 %copy-start.8 = (bf16[4,128,256]{2,1,0:T(8,128)(2,1)}, bf16[4,128,256]{2,1,0:T(8,128)(2,1)S(1)}, u32[]{:S(2)}) copy-start(bf16[4,128,256]{2,1,0:T(8,128)(2,1)S(1)} %collective-permute-done.2.refs_1_) | copy-start | bytes 786436
  105.6 15.0 %collective-permute-start.6 = (bf16[4,128,256]{2,1,0:T(8,128)(2,1)S(1)}, bf16[4,128,256]{2,1,0:T(8,128)(2,1)S(1)}, u32[]{:S(2)}, u32[]{:S(2)}) collective-permute-start(bf16[4,128,256]{2,1,0:T(8,128)(2,1)S(1)} %bitcast.57), channel_id=1, source_target_pairs={{0,80},{16,96},{32,112},{48,64},{64,16},{80,32},{96,48},{112,0},{1... | collective-permute-start | bytes 786440 | tf_op jit(solution)/shard_map/ppermute | solution.py:229
  105.8 30.6 %copy-start.9 = (bf16[4,128,256]{2,1,0:T(8,128)(2,1)}, bf16[4,128,256]{2,1,0:T(8,128)(2,1)S(1)}, u32[]{:S(2)}) copy-start(bf16[4,128,256]{2,1,0:T(8,128)(2,1)S(1)} %collective-permute-done.3.refs_2_) | copy-start | bytes 786436
  105.8 16.2 %collective-permute-start.7 = (bf16[4,128,256]{2,1,0:T(8,128)(2,1)S(1)}, bf16[4,128,256]{2,1,0:T(8,128)(2,1)S(1)}, u32[]{:S(2)}, u32[]{:S(2)}) collective-permute-start(bf16[4,128,256]{2,1,0:T(8,128)(2,1)S(1)} %bitcast.58), channel_id=1, source_target_pairs={{0,96},{16,112},{32,64},{48,80},{64,32},{80,48},{96,0},{112,16},{1... | collective-permute-start | bytes 786440 | tf_op jit(solution)/shard_map/ppermute | solution.py:229
  108.9 13.1 %collective-permute-start.8 = (bf16[4,128,256]{2,1,0:T(8,128)(2,1)S(1)}, bf16[4,128,256]{2,1,0:T(8,128)(2,1)S(1)}, u32[]{:S(2)}, u32[]{:S(2)}) collective-permute-start(bf16[4,128,256]{2,1,0:T(8,128)(2,1)S(1)} %bitcast.59), channel_id=1, source_target_pairs={{0,112},{16,64},{32,80},{48,96},{64,48},{80,0},{96,16},{112,32},{1... | collective-permute-start | bytes 786440 | tf_op jit(solution)/shard_map/ppermute | solution.py:229
  111.3 10.7 %copy-start.10 = (bf16[4,128,256]{2,1,0:T(8,128)(2,1)}, bf16[4,128,256]{2,1,0:T(8,128)(2,1)S(1)}, u32[]{:S(2)}) copy-start(bf16[4,128,256]{2,1,0:T(8,128)(2,1)S(1)} %collective-permute-done.5.refs_4_) | copy-start | bytes 786436
  111.3 16.3 %collective-permute-start.9 = (bf16[4,128,256]{2,1,0:T(8,128)(2,1)S(1)}, bf16[4,128,256]{2,1,0:T(8,128)(2,1)}, u32[]{:S(2)}, u32[]{:S(2)}) collective-permute-start(bf16[4,128,256]{2,1,0:T(8,128)(2,1)S(1)} %bitcast.60), channel_id=1, source_target_pairs={{0,8},{8,0},{1,9},{9,1},{2,10},{10,2},{3,11},{11,3},{4,12},{12,4},... | collective-permute-start | bytes 786440 | tf_op jit(solution)/shard_map/ppermute | solution.py:230
  120.6 1.5 copy-start.11
  120.6 7.6 %collective-permute-start.10 = (bf16[4,128,256]{2,1,0:T(8,128)(2,1)S(1)}, bf16[4,128,256]{2,1,0:T(8,128)(2,1)}, u32[]{:S(2)}, u32[]{:S(2)}) collective-permute-start(bf16[4,128,256]{2,1,0:T(8,128)(2,1)S(1)} %collective-permute-done.2.refs_1_), channel_id=1, source_target_pairs={{0,8},{8,0},{1,9},{9,1},{2,10},{10,2},{3,11},{11,3},{4,12},{12,4},... | collective-permute-start | bytes 786440 | tf_op jit(solution)/shard_map/ppermute | solution.py:230
  122.0 0.7 copy-start.12
  122.0 6.4 %collective-permute-start.11 = (bf16[4,128,256]{2,1,0:T(8,128)(2,1)S(1)}, bf16[4,128,256]{2,1,0:T(8,128)(2,1)}, u32[]{:S(2)}, u32[]{:S(2)}) collective-permute-start(bf16[4,128,256]{2,1,0:T(8,128)(2,1)S(1)} %collective-permute-done.3.refs_2_), channel_id=1, source_target_pairs={{0,8},{8,0},{1,9},{9,1},{2,10},{10,2},{3,11},{11,3},{4,12},{12,4},... | collective-permute-start | bytes 786440 | tf_op jit(solution)/shard_map/ppermute | solution.py:230
  123.4 5.3 %collective-permute-start.12 = (bf16[4,128,256]{2,1,0:T(8,128)(2,1)}, bf16[4,128,256]{2,1,0:T(8,128)(2,1)}, u32[]{:S(2)}, u32[]{:S(2)}) collective-permute-start(bf16[4,128,256]{2,1,0:T(8,128)(2,1)} %collective-permute-done.4.refs_3_), channel_id=1, source_target_pairs={{0,8},{8,0},{1,9},{9,1},{2,10},{10,2},{3,11},{11,3},{4,12},{12,4},... | collective-permute-start | bytes 786440 | tf_op jit(solution)/shard_map/ppermute | solution.py:230
  124.1 12.3 %all-to-all-start.4 = ((bf16[8,2,16,640]{3,2,1,0:T(8,128)(2,1)}), bf16[8,2,16,640]{3,2,1,0:T(8,128)(2,1)S(1)}, u32[]{:S(2)}, u32[]{:S(2)}) async-start(bf16[8,2,16,640]{3,2,1,0:T(8,128)(2,1)} %broadcast_in_dim.109), calls=%async_computation.4 | async-start | bytes 655360 | tf_op jit(solution)/shard_map/all_to_all | solution.py:29
  127.6 4.6 %collective-permute-start.13 = (bf16[4,128,256]{2,1,0:T(8,128)(2,1)}, bf16[4,128,256]{2,1,0:T(8,128)(2,1)S(1)}, u32[]{:S(2)}, u32[]{:S(2)}) collective-permute-start(bf16[4,128,256]{2,1,0:T(8,128)(2,1)} %copy-done.10), channel_id=1, source_target_pairs={{0,8},{8,0},{1,9},{9,1},{2,10},{10,2},{3,11},{11,3},{4,12},{12,4},... | collective-permute-start | bytes 786440 | tf_op jit(solution)/shard_map/ppermute | solution.py:230
  128.2 4.0 %collective-permute-start.14 = (bf16[4,128,256]{2,1,0:T(8,128)(2,1)}, bf16[4,128,256]{2,1,0:T(8,128)(2,1)S(1)}, u32[]{:S(2)}, u32[]{:S(2)}) collective-permute-start(bf16[4,128,256]{2,1,0:T(8,128)(2,1)} %copy-done.11), channel_id=1, source_target_pairs={{0,8},{8,0},{1,9},{9,1},{2,10},{10,2},{3,11},{11,3},{4,12},{12,4},... | collective-permute-start | bytes 786440 | tf_op jit(solution)/shard_map/ppermute | solution.py:230
  128.5 3.7 %collective-permute-start.15 = (bf16[4,128,256]{2,1,0:T(8,128)(2,1)}, bf16[4,128,256]{2,1,0:T(8,128)(2,1)S(1)}, u32[]{:S(2)}, u32[]{:S(2)}) collective-permute-start(bf16[4,128,256]{2,1,0:T(8,128)(2,1)} %copy-done.12), channel_id=1, source_target_pairs={{0,8},{8,0},{1,9},{9,1},{2,10},{10,2},{3,11},{11,3},{4,12},{12,4},... | collective-permute-start | bytes 786440 | tf_op jit(solution)/shard_map/ppermute | solution.py:230
  128.7 4.2 %collective-permute-start.16 = (bf16[4,128,256]{2,1,0:T(8,128)(2,1)}, bf16[4,128,256]{2,1,0:T(8,128)(2,1)}, u32[]{:S(2)}, u32[]{:S(2)}) collective-permute-start(bf16[4,128,256]{2,1,0:T(8,128)(2,1)} %copy-done.13), channel_id=1, source_target_pairs={{0,8},{8,0},{1,9},{9,1},{2,10},{10,2},{3,11},{11,3},{4,12},{12,4},... | collective-permute-start | bytes 786440 | tf_op jit(solution)/shard_map/ppermute | solution.py:230
  132.2 4.3 %copy-start.14 = (bf16[4,128,256]{2,1,0:T(8,128)(2,1)}, bf16[4,128,256]{2,1,0:T(8,128)(2,1)S(1)}, u32[]{:S(2)}) copy-start(bf16[4,128,256]{2,1,0:T(8,128)(2,1)S(1)} %collective-permute-done.13.refs_12_) | copy-start | bytes 786436
  132.2 4.3 %copy-start.15 = (bf16[4,128,256]{2,1,0:T(8,128)(2,1)}, bf16[4,128,256]{2,1,0:T(8,128)(2,1)S(1)}, u32[]{:S(2)}) copy-start(bf16[4,128,256]{2,1,0:T(8,128)(2,1)S(1)} %collective-permute-done.14.refs_13_) | copy-start | bytes 786436
  132.2 0.7 copy-start.16
  136.5 0.7 copy-start.2
  151.3 13.9 %collective-permute-start.17 = (bf16[2048,128]{1,0:T(8,128)(2,1)}, bf16[2048,128]{1,0:T(8,128)(2,1)}, u32[]{:S(2)}, u32[]{:S(2)}) collective-permute-start(bf16[2048,128]{1,0:T(8,128)(2,1)} %moved.1.refs_0_), channel_id=1, source_target_pairs={{0,4},{4,0},{1,5},{5,1},{2,6},{6,2},{3,7},{7,3},{8,12},{12,8},{9,1... | collective-permute-start | bytes 1572872 | tf_op jit(solution)/shard_map/ppermute | solution.py:263
  151.9 15.4 %collective-permute-start.20 = (bf16[2048,128]{1,0:T(8,128)(2,1)}, bf16[2048,128]{1,0:T(8,128)(2,1)}, u32[]{:S(2)}, u32[]{:S(2)}) collective-permute-start(bf16[2048,128]{1,0:T(8,128)(2,1)} %moved.1.refs_0_), channel_id=1, source_target_pairs={{0,1},{1,2},{2,3},{3,0},{4,5},{5,6},{6,7},{7,4},{8,9},{9,10},{10,1... | collective-permute-start | bytes 1572872 | tf_op jit(solution)/shard_map/ppermute | solution.py:264
  152.8 15.0 %collective-permute-start.21 = (bf16[2048,128]{1,0:T(8,128)(2,1)}, bf16[2048,128]{1,0:T(8,128)(2,1)}, u32[]{:S(2)}, u32[]{:S(2)}) collective-permute-start(bf16[2048,128]{1,0:T(8,128)(2,1)} %moved.1.refs_0_), channel_id=1, source_target_pairs={{0,3},{1,0},{2,1},{3,2},{4,7},{5,4},{6,5},{7,6},{8,11},{9,8},{10,9... | collective-permute-start | bytes 1572872 | tf_op jit(solution)/shard_map/ppermute | solution.py:265
  165.3 13.2 %collective-permute-start.18 = (bf16[2048,128]{1,0:T(8,128)(2,1)}, bf16[2048,128]{1,0:T(8,128)(2,1)S(1)}, u32[]{:S(2)}, u32[]{:S(2)}) collective-permute-start(bf16[2048,128]{1,0:T(8,128)(2,1)} %collective-permute-done.17.refs_1_), channel_id=1, source_target_pairs={{0,3},{1,0},{2,1},{3,2},{4,7},{5,4},{6,5},{7,6},{8,11},{9,8},{10,9... | collective-permute-start | bytes 1572872 | tf_op jit(solution)/shard_map/ppermute | solution.py:267
  165.5 23.9 %collective-permute-start.30 = (bf16[2048,128]{1,0:T(8,128)(2,1)}, bf16[2048,128]{1,0:T(8,128)(2,1)S(1)}, u32[]{:S(2)}, u32[]{:S(2)}) collective-permute-start(bf16[2048,128]{1,0:T(8,128)(2,1)} %collective-permute-done.17.refs_1_), channel_id=1, source_target_pairs={{0,1},{1,2},{2,3},{3,0},{4,5},{5,6},{6,7},{7,4},{8,9},{9,10},{10,1... | collective-permute-start | bytes 1572872 | tf_op jit(solution)/shard_map/ppermute | solution.py:266
  167.3 25.3 %collective-permute-start.31 = (bf16[2048,128]{1,0:T(8,128)(2,1)}, bf16[2048,128]{1,0:T(8,128)(2,1)}, u32[]{:S(2)}, u32[]{:S(2)}) collective-permute-start(bf16[2048,128]{1,0:T(8,128)(2,1)} %collective-permute-done.20.refs_2_), channel_id=1, source_target_pairs={{0,1},{1,2},{2,3},{3,0},{4,5},{5,6},{6,7},{7,4},{8,9},{9,10},{10,1... | collective-permute-start | bytes 1572872 | tf_op jit(solution)/shard_map/ppermute | solution.py:268
  178.5 18.3 %copy-start.4 = (bf16[2048,128]{1,0:T(8,128)(2,1)}, bf16[2048,128]{1,0:T(8,128)(2,1)S(1)}, u32[]{:S(2)}) copy-start(bf16[2048,128]{1,0:T(8,128)(2,1)S(1)} %collective-permute-done.18.refs_1_) | copy-start | bytes 1572868
  178.5 16.2 %collective-permute-start.32 = (bf16[2048,128]{1,0:T(8,128)(2,1)S(1)}, bf16[2048,128]{1,0:T(8,128)(2,1)S(1)}, u32[]{:S(2)}, u32[]{:S(2)}) collective-permute-start(bf16[2048,128]{1,0:T(8,128)(2,1)S(1)} %collective-permute-done.18.refs_1_), channel_id=1, source_target_pairs={{0,3},{1,0},{2,1},{3,2},{4,7},{5,4},{6,5},{7,6},{8,11},{9,8},{10,9... | collective-permute-start | bytes 1572872 | tf_op jit(solution)/shard_map/ppermute | solution.py:271
  181.6 28.8 %collective-permute-start.22 = (bf16[288,512]{1,0:T(8,128)(2,1)}, bf16[288,512]{1,0:T(8,128)(2,1)}, u32[]{:S(2)}, u32[]{:S(2)}) collective-permute-start(bf16[288,512]{1,0:T(8,128)(2,1)} %get-tuple-element.76), channel_id=1, source_target_pairs={{0,32},{16,48},{32,0},{48,16},{64,96},{80,112},{96,64},{112,80},{1... | collective-permute-start | bytes 884744 | tf_op jit(solution)/shard_map/ppermute | solution.py:278
  189.3 24.4 %collective-permute-start.23 = (bf16[288,512]{1,0:T(8,128)(2,1)}, bf16[288,512]{1,0:T(8,128)(2,1)}, u32[]{:S(2)}, u32[]{:S(2)}) collective-permute-start(bf16[288,512]{1,0:T(8,128)(2,1)} %get-tuple-element.77), channel_id=1, source_target_pairs={{0,16},{16,32},{32,48},{48,0},{64,80},{80,96},{96,112},{112,64},{1... | collective-permute-start | bytes 884744 | tf_op jit(solution)/shard_map/ppermute | solution.py:278
  189.4 7.4 %copy-start.5 = (bf16[2048,128]{1,0:T(8,128)(2,1)}, bf16[2048,128]{1,0:T(8,128)(2,1)S(1)}, u32[]{:S(2)}) copy-start(bf16[2048,128]{1,0:T(8,128)(2,1)S(1)} %collective-permute-done.30.refs_0_) | copy-start | bytes 1572868
  189.4 29.3 %collective-permute-start.24 = (bf16[288,512]{1,0:T(8,128)(2,1)}, bf16[288,512]{1,0:T(8,128)(2,1)}, u32[]{:S(2)}, u32[]{:S(2)}) collective-permute-start(bf16[288,512]{1,0:T(8,128)(2,1)} %get-tuple-element.78), channel_id=1, source_target_pairs={{0,48},{16,0},{32,16},{48,32},{64,112},{80,64},{96,80},{112,96},{1... | collective-permute-start | bytes 884744 | tf_op jit(solution)/shard_map/ppermute | solution.py:278
  192.6 26.1 %collective-permute-start.25 = (bf16[288,512]{1,0:T(8,128)(2,1)}, bf16[288,512]{1,0:T(8,128)(2,1)S(1)}, u32[]{:S(2)}, u32[]{:S(2)}) collective-permute-start(bf16[288,512]{1,0:T(8,128)(2,1)} %get-tuple-element.81), channel_id=1, source_target_pairs={{0,96},{16,112},{32,64},{48,80},{64,32},{80,48},{96,0},{112,16},{1... | collective-permute-start | bytes 884744 | tf_op jit(solution)/shard_map/ppermute | solution.py:278
  194.7 0.8 copy-start.6
  195.5 23.3 %collective-permute-start.26 = (bf16[288,512]{1,0:T(8,128)(2,1)}, bf16[288,512]{1,0:T(8,128)(2,1)}, u32[]{:S(2)}, u32[]{:S(2)}) collective-permute-start(bf16[288,512]{1,0:T(8,128)(2,1)} %get-tuple-element.82), channel_id=1, source_target_pairs={{0,80},{16,96},{32,112},{48,64},{64,16},{80,32},{96,48},{112,0},{1... | collective-permute-start | bytes 884744 | tf_op jit(solution)/shard_map/ppermute | solution.py:278
  210.5 13.0 %collective-permute-start.27 = (bf16[288,512]{1,0:T(8,128)(2,1)}, bf16[288,512]{1,0:T(8,128)(2,1)S(1)}, u32[]{:S(2)}, u32[]{:S(2)}) collective-permute-start(bf16[288,512]{1,0:T(8,128)(2,1)} %get-tuple-element.83), channel_id=1, source_target_pairs={{0,112},{16,64},{32,80},{48,96},{64,48},{80,0},{96,16},{112,32},{1... | collective-permute-start | bytes 884744 | tf_op jit(solution)/shard_map/ppermute | solution.py:278
  213.7 19.7 %collective-permute-start.28 = (bf16[288,512]{1,0:T(8,128)(2,1)}, bf16[288,512]{1,0:T(8,128)(2,1)S(1)}, u32[]{:S(2)}, u32[]{:S(2)}) collective-permute-start(bf16[288,512]{1,0:T(8,128)(2,1)} %get-tuple-element.84), channel_id=1, source_target_pairs={{0,64},{16,80},{32,96},{48,112},{64,0},{80,16},{96,32},{112,48},{1... | collective-permute-start | bytes 884744 | tf_op jit(solution)/shard_map/ppermute | solution.py:278
  218.7 22.1 %collective-permute-start.33 = (bf16[288,512]{1,0:T(8,128)(2,1)}, bf16[288,512]{1,0:T(8,128)(2,1)}, u32[]{:S(2)}, u32[]{:S(2)}) collective-permute-start(bf16[288,512]{1,0:T(8,128)(2,1)} %get-tuple-element.93), channel_id=1, source_target_pairs={{0,32},{16,48},{32,0},{48,16},{64,96},{80,112},{96,64},{112,80},{1... | collective-permute-start | bytes 884744 | tf_op jit(solution)/shard_map/ppermute | solution.py:278
  218.7 26.3 %collective-permute-start.34 = (bf16[288,512]{1,0:T(8,128)(2,1)}, bf16[288,512]{1,0:T(8,128)(2,1)}, u32[]{:S(2)}, u32[]{:S(2)}) collective-permute-start(bf16[288,512]{1,0:T(8,128)(2,1)} %get-tuple-element.94), channel_id=1, source_target_pairs={{0,16},{16,32},{32,48},{48,0},{64,80},{80,96},{96,112},{112,64},{1... | collective-permute-start | bytes 884744 | tf_op jit(solution)/shard_map/ppermute | solution.py:278
  218.8 27.2 %copy-start.7 = (bf16[288,512]{1,0:T(8,128)(2,1)S(1)}, bf16[288,512]{1,0:T(8,128)(2,1)}, u32[]{:S(2)}) copy-start(bf16[288,512]{1,0:T(8,128)(2,1)} %get-tuple-element.96) | copy-start | bytes 884740
  218.8 27.1 %collective-permute-start.35 = (bf16[288,512]{1,0:T(8,128)(2,1)}, bf16[288,512]{1,0:T(8,128)(2,1)S(1)}, u32[]{:S(2)}, u32[]{:S(2)}) collective-permute-start(bf16[288,512]{1,0:T(8,128)(2,1)} %get-tuple-element.95), channel_id=1, source_target_pairs={{0,48},{16,0},{32,16},{48,32},{64,112},{80,64},{96,80},{112,96},{1... | collective-permute-start | bytes 884744 | tf_op jit(solution)/shard_map/ppermute | solution.py:278
  223.5 23.9 %collective-permute-start.36 = (bf16[288,512]{1,0:T(8,128)(2,1)}, bf16[288,512]{1,0:T(8,128)(2,1)S(1)}, u32[]{:S(2)}, u32[]{:S(2)}) collective-permute-start(bf16[288,512]{1,0:T(8,128)(2,1)} %get-tuple-element.98), channel_id=1, source_target_pairs={{0,96},{16,112},{32,64},{48,80},{64,32},{80,48},{96,0},{112,16},{1... | collective-permute-start | bytes 884744 | tf_op jit(solution)/shard_map/ppermute | solution.py:278
  233.4 14.0 %collective-permute-start.37 = (bf16[288,512]{1,0:T(8,128)(2,1)}, bf16[288,512]{1,0:T(8,128)(2,1)S(1)}, u32[]{:S(2)}, u32[]{:S(2)}) collective-permute-start(bf16[288,512]{1,0:T(8,128)(2,1)} %get-tuple-element.99), channel_id=1, source_target_pairs={{0,80},{16,96},{32,112},{48,64},{64,16},{80,32},{96,48},{112,0},{1... | collective-permute-start | bytes 884744 | tf_op jit(solution)/shard_map/ppermute | solution.py:278
  240.8 10.4 %collective-permute-start.38 = (bf16[288,512]{1,0:T(8,128)(2,1)}, bf16[288,512]{1,0:T(8,128)(2,1)S(1)}, u32[]{:S(2)}, u32[]{:S(2)}) collective-permute-start(bf16[288,512]{1,0:T(8,128)(2,1)} %get-tuple-element.100), channel_id=1, source_target_pairs={{0,112},{16,64},{32,80},{48,96},{64,48},{80,0},{96,16},{112,32},{1... | collective-permute-start | bytes 884744 | tf_op jit(solution)/shard_map/ppermute | solution.py:278
  244.9 10.3 %collective-permute-start.39 = (bf16[288,512]{1,0:T(8,128)(2,1)}, bf16[288,512]{1,0:T(8,128)(2,1)S(1)}, u32[]{:S(2)}, u32[]{:S(2)}) collective-permute-start(bf16[288,512]{1,0:T(8,128)(2,1)} %get-tuple-element.101), channel_id=1, source_target_pairs={{0,64},{16,80},{32,96},{48,112},{64,0},{80,16},{96,32},{112,48},{1... | collective-permute-start | bytes 884744 | tf_op jit(solution)/shard_map/ppermute | solution.py:278
  245.9 11.4 %collective-permute-start.29 = (f32[144,512]{1,0:T(8,128)S(1)}, f32[144,512]{1,0:T(8,128)}, u32[]{:S(2)}, u32[]{:S(2)}) collective-permute-start(f32[144,512]{1,0:T(8,128)S(1)} %add_add_fusion.3), channel_id=1, source_target_pairs={{0,8},{8,0},{1,9},{9,1},{2,10},{10,2},{3,11},{11,3},{4,12},{12,4},... | collective-permute-start | bytes 884744 | tf_op jit(solution)/shard_map/ppermute | solution.py:290
  255.3 2.0 collective-permute-start.40
  (1 other events, 0.7 us)

commit v2 on v1

--- a/solution.py
+++ b/solution.py
@@ -30,10 +30,10 @@
 
 
 def moved_kernel(where_ref, bound_ref, tiles_ref, *refs):
-    pieces = refs[:16]
-    out_ref, acc_ref, eo_ref, ev_ref, oe_ref, ve_ref, win_ref, all_ref, sems = refs[16:]
+    pieces = refs[:8]
+    out_ref, acc_ref, eo_ref, ev_ref, oe_ref, ve_ref, win_ref, all_ref, sems = refs[8:]
     copies = [
-        pltpu.make_async_copy(piece, all_ref.at[pl.ds(n * OWN, OWN)], sems.at[n])
+        pltpu.make_async_copy(piece, all_ref.at[pl.ds(n * CHIP, CHIP)], sems.at[n])
         for n, piece in enumerate(pieces)
     ]
     for copy in copies:
@@ -71,7 +71,7 @@
             acc_ref[s] = total
             return c
 
-        return lax.fori_loop(0, CHIP, target, carry, unroll=4)
+        return lax.fori_loop(0, CHIP, target, carry, unroll=8)
 
     lax.fori_loop(0, LIVE // 8, group, 0)
     for s in range(CHIP):
@@ -85,7 +85,7 @@
     return pl.pallas_call(
         moved_kernel,
         out_shape=jax.ShapeDtypeStruct((CHIP * TILE, WIN_DEV), BF16),
-        in_specs=[sm, sm, vm] + [pl.BlockSpec(memory_space=pl.ANY)] * 16,
+        in_specs=[sm, sm, vm] + [pl.BlockSpec(memory_space=pl.ANY)] * 8,
         out_specs=vm,
         scratch_shapes=[
             pltpu.VMEM((CHIP, WIN_DEV, TILE), F32),
@@ -95,7 +95,7 @@
             pltpu.VMEM((128, 2048), F32),
             pltpu.VMEM((8, WIN_DEV, TILE), BF16),
             pltpu.VMEM((16 * OWN, WIN_DEV, TILE), BF16),
-            pltpu.SemaphoreType.DMA((16,)),
+            pltpu.SemaphoreType.DMA((8,)),
         ],
         name="moved",
     )(where, bounds, tiles, *pieces)
@@ -173,6 +173,8 @@
     aux_rows = three_center.shape[0]
     chip_rows = aux_rows // 8
 
+    window = jnp.transpose(three_center[:WIN_DEV], (1, 0, 2))
+    paired = lax.ppermute(window, "yh", SWAP)
     facts = jnp.concatenate([pair_blocks.reshape(-1), block_count])
     facts = jnp.pad(facts, (0, 128 - facts.shape[0]))
     facts = jnp.broadcast_to(facts[None], (8, 128))
@@ -190,8 +192,8 @@
     chosen = jnp.arange(LIVE, dtype=jnp.int32)[:, None] == slot_rank[None, :]
     sg = slots // OWN
     place_of = (
-        jnp.where(sg % 2 == c, 0, 8 * OWN)
-        + (((y - sg // 8) % 2) * 4 + (z - (sg // 2) % 4) % 4) * OWN + slot_in)
+        jnp.where(sg % 2 == c, 0, 8 * OWN) + ((z - (sg // 2) % 4) % 4) * CHIP
+        + jnp.where(sg // 8 == y, 0, OWN) + slot_in)
     where = jnp.sum(jnp.where(chosen, place_of[None, :], 0), axis=1)
     live_names = jnp.sum(jnp.where(chosen[:, :, None], names[None], 0), axis=1)
 
@@ -223,10 +225,11 @@
     kept = kept + given
     kept = lax.all_to_all(kept.reshape(8, -1, n_half), ZY, 0, 0)
     mine = three_center.reshape(aux_rows, OWN * TILE)
-    window = jnp.transpose(three_center[:WIN_DEV], (1, 0, 2))
     tau = jnp.sum(jnp.where(jnp.arange(2) == c, tau_points, 0.0), keepdims=True)
-    kept, mine, window, tau = lax.optimization_barrier((kept, mine, window, tau))
-    near = [window] + [lax.ppermute(window, ZY, shift_zy(i)) for i in range(1, 8)]
+    packed = jnp.concatenate([window, paired])
+    kept, mine, packed, tau = lax.optimization_barrier((kept, mine, packed, tau))
+    near = [packed] + [
+        lax.ppermute(packed, "z", [(n, (n + i) % 4) for n in range(4)]) for i in range(1, 4)]
     windows = near + [lax.ppermute(piece, "c", SWAP) for piece in near]
     kept = jnp.sum(kept.astype(F32), axis=0).astype(BF16)
     kept = spread(kept, ZY, 8).reshape(LIVE * BS, n_half)

time: 263 us -> 257 us (0.977)
  starting transfers between devices: 66.6 us -> 56.8 us
  waiting for transfers between devices: 79.5 us -> 87 us
  local copies, waits for them, and re-layouts: 16.8 us -> 13.6 us
    ppermute x7 -> x4, waiting for transfers between devices: 21.3 us -> 33.7 us  [the longest x3 23.4 us: step(): lax.ppermute(packed, 'z', [(n, (n + i) % 4) for n in range(4)])]
    all_to_all x1, waiting for transfers between devices: 7.51 us -> 0.01 us  [step(): kept = lax.all_to_all(kept.reshape(8, -1, n_half), ZY, 0, 0)]
    ppermute x14, starting transfers between devices: 29.6 us -> 23.9 us  [step(): sums.append(lax.ppermute(part, ZY, shift_zy(i)) if i else part)]
    ppermute x1, waiting for transfers between devices: 0.01 us -> 5.19 us  [step(): bpp = lax.ppermute(bp, 'x', XP)]
    ppermute x14, waiting for transfers between devices: 28.5 us -> 24.1 us  [step(): sums.append(lax.ppermute(part, ZY, shift_zy(i)) if i else part)]
    ppermute x7 -> x4, starting transfers between devices: 10.5 us -> 7.07 us  [the longest x3 3.56 us: step(): lax.ppermute(packed, 'z', [(n, (n + i) % 4) for n in range(4)])]
    unnamed x45 -> x27, local copies, waits for them, and re-layouts: 10.6 us -> 8.53 us
  transfers between devices with their start and end apart: 44 -> 37, of which waited for: 17 -> 14; matrix products, arithmetic and copies ran while one was open for 8% -> 8% of each run, Pallas kernels for 14% -> 14%
where the time goes in v2:
time: 257 us; the launch traced here: 255 us
  waiting for transfers between devices  87 us (34%)
  starting transfers between devices  56.8 us (22%)
  Pallas kernels  37.9 us (15%)
  blocking collectives  36.7 us (14%)
  other arithmetic  16.7 us (6%)
  local copies, waits for them, and re-layouts  13.6 us (5%)
  matrix products  3.11 us (1%)
  between operations  2.98 us (1%)
    ppermute x14, waiting for transfers between devices, step(): sums.append(lax.ppermute(part, ZY, shift_zy(i)) if i else part)  24.1 us
    ppermute x14, starting transfers between devices, step(): sums.append(lax.ppermute(part, ZY, shift_zy(i)) if i else part)  23.9 us
    ppermute x3, waiting for transfers between devices, step(): lax.ppermute(packed, 'z', [(n, (n + i) % 4) for n in range(4)])  23.4 us
    pallas_call x2, Pallas kernels, partial_rows(): pl.pallas_call(partial_kernel, out_shape=[jax.ShapeDtypeStruct((rows, 4 *...  21.3 us
    all_to_all x1, blocking collectives, spread(): lax.all_to_all(jnp.broadcast_to(x[None], (count,) + x.shape), axes, 0, 0)  20 us
    all_to_all x1, blocking collectives, step(): grams = jnp.sum(lax.all_to_all(grams, AUX, 0, 0), axis=0)  16.7 us
    pallas_call x1, Pallas kernels, moved_blocks(): pl.pallas_call(moved_kernel, out_shape=jax.ShapeDtypeStruct((CHIP * TILE,...  13.6 us
    all_to_all x2, waiting for transfers between devices, spread(): lax.all_to_all(jnp.broadcast_to(x[None], (count,) + x.shape), axes, 0, 0)  13 us
  transfers between devices with their start and end apart: 37, of which 14 were waited for; matrix products, arithmetic and copies ran while one was open for 8% of the time, Pallas kernels for 14%

profile of v2, /device:TPU:0, one launch (start us, length us, event | category | flops | bytes accessed | tf_op | source)
XLA Modules:
  0.0 254.8 jit_solution(1461982244088113447)
XLA Ops:
  0.0 0.9 copy.23
  1.7 0.6 broadcast_in_dim_broadcast_in_dim_broadcast_in_dim.2
  2.4 8.2 %all-to-all-start = ((s32[16,8,128]{2,1,0:T(8,128)}), s32[16,8,128]{2,1,0:T(8,128)S(1)}, u32[]{:S(2)}, u32[]{:S(2)}) async-start(s32[16,8,128]{2,1,0:T(8,128)} %broadcast_in_dim_broadcast_in_dim_broadcast_in_dim.2), calls=%async_computation | async-start | bytes 131072 | tf_op jit(solution)/shard_map/all_to_all | solution.py:29
  10.7 7.6 %all-to-all-done = s32[16,8,128]{2,1,0:T(8,128)S(1)} async-done(((s32[16,8,128]{2,1,0:T(8,128)}), s32[16,8,128]{2,1,0:T(8,128)S(1)}, u32[]{:S(2)}, u32[]{:S(2)}) %all-to-all-start) | async-done | bytes 65568 | tf_op jit(solution)/shard_map/all_to_all | solution.py:29
  19.4 1.7 convolution_convert_fusion
  21.7 1.2 broadcast_select_fusion.2
  22.9 0.7 stack.85.dest_ref
  23.6 0.6 stack.76.place_ref
  24.2 0.7 fusion.23
  24.9 0.8 collective-permute-done
  25.6 2.8 %select_add_fusion = bf16[640,768]{1,0:T(8,128)(2,1)} fusion(bf16[640,768]{1,0:T(8,128)(2,1)S(1)} %collective-permute-done, pred[]{:T(512)S(6)} %eq.104, bf16[640,1408]{1,0:T(8,128)(2,1)} %copy-done.1, bf16[640,128]{1,0:T(8,128)(2,1)S(1)} %fusion.3), kind=kLoop, calls=%fused_computation.11 | loop fusion | flops 4423680 | bytes 4915201 | tf_op jit(solution)/shard_map/add | solution.py:225
  28.4 3.7 %all-to-all-start.1 = ((bf16[8,80,768]{2,1,0:T(8,128)(2,1)}), bf16[8,80,768]{2,1,0:T(8,128)(2,1)S(1)}, u32[]{:S(2)}, u32[]{:S(2)}) async-start(bf16[8,80,768]{2,1,0:T(8,128)(2,1)} %bitcast.22), calls=%async_computation.1 | async-start | bytes 1966080 | tf_op jit(solution)/shard_map/all_to_all | solution.py:226
  32.1 3.5 %collective-permute-start.1 = (bf16[4,128,256]{2,1,0:T(8,128)(2,1)S(1)}, bf16[4,128,256]{2,1,0:T(8,128)(2,1)S(1)}, u32[]{:S(2)}, u32[]{:S(2)}) collective-permute-start(bf16[4,128,256]{2,1,0:T(8,128)(2,1)S(1)} %bitcast.53), channel_id=1, source_target_pairs={{0,64},{64,0},{1,65},{65,1},{2,66},{66,2},{3,67},{67,3},{4,68},{68... | collective-permute-start | bytes 786440 | tf_op jit(solution)/shard_map/ppermute | solution.py:177
  35.7 6.0 %copy.31 = bf16[288,8,4,256]{3,1,2,0:T(8,128)(2,1)} copy(bf16[288,8,4,256]{3,2,1,0:T(4,128)(2,1)} %bitcast.50) | data formatting | bytes 9437184
  41.7 0.7 fusion.16
  42.3 10.3 %collective-permute-done.1 = bf16[4,128,256]{2,1,0:T(8,128)(2,1)S(1)} collective-permute-done((bf16[4,128,256]{2,1,0:T(8,128)(2,1)S(1)}, bf16[4,128,256]{2,1,0:T(8,128)(2,1)S(1)}, u32[]{:S(2)}, u32[]{:S(2)}) %collective-permute-start.1) | collective-permute-done | bytes 262176 | tf_op jit(solution)/shard_map/ppermute | solution.py:177
  52.6 0.8 pad_maximum_fusion.1.refs_0_
  53.7 20.0 %all_to_all.25 = bf16[8,80,768]{2,1,0:T(8,128)(2,1)S(1)} all-to-all(bf16[8,80,768]{2,1,0:T(8,128)(2,1)S(1)} %broadcast_in_dim.110), channel_id=1, replica_groups=mesh['yh'=2,'z'=4,'c'=2,'yl'=2,'x'=4] {'yh','z'}, dimensions={0} | all-to-all | bytes 1966080 | tf_op jit(solution)/shard_map/all_to_all | solution.py:29
  75.6 0.6 multiply_exponential_fusion.1
  76.4 1.3 broadcast_select_fusion.1
  78.4 0.7 fusion.1
  79.1 16.7 %all_to_all.26 = f32[8,2,16,640]{3,2,1,0:T(8,128)S(1)} all-to-all(f32[8,2,16,640]{3,2,1,0:T(8,128)S(1)} %maximum_bitcast_fusion), channel_id=1, replica_groups=mesh['yh'=2,'z'=4,'c'=2,'yl'=2,'x'=4] {'yl','x'}, dimensions={0} | all-to-all | bytes 1310720 | tf_op jit(solution)/shard_map/all_to_all | solution.py:255
  96.4 2.1 collective-permute-start.4
  98.5 1.1 collective-permute-start.5
  99.6 23.3 %collective-permute-done.3.refs_1_ = bf16[8,128,256]{2,1,0:T(8,128)(2,1)} collective-permute-done((bf16[8,128,256]{2,1,0:T(8,128)(2,1)S(1)}, bf16[8,128,256]{2,1,0:T(8,128)(2,1)}, u32[]{:S(2)}, u32[]{:S(2)}) %collective-permute-start.3) | collective-permute-done | bytes 524320 | tf_op jit(solution)/shard_map/ppermute | solution.py:232
  123.5 0.8 broadcast_in_dim.111
  124.2 3.6 %all-to-all-start.4 = ((bf16[8,2,16,640]{3,2,1,0:T(8,128)(2,1)}), bf16[8,2,16,640]{3,2,1,0:T(8,128)(2,1)S(1)}, u32[]{:S(2)}, u32[]{:S(2)}) async-start(bf16[8,2,16,640]{3,2,1,0:T(8,128)(2,1)} %broadcast_in_dim.111), calls=%async_computation.4 | async-start | bytes 655360 | tf_op jit(solution)/shard_map/all_to_all | solution.py:29
  128.5 1.9 pad_add_fusion.1.bound_ref
  130.4 0.6 select_reduce_fusion.1.where_ref
  131.1 5.5 %all-to-all-done.4.tiles_ref = bf16[8,2,16,640]{3,2,1,0:T(8,128)(2,1)S(1)} async-done(((bf16[8,2,16,640]{3,2,1,0:T(8,128)(2,1)}), bf16[8,2,16,640]{3,2,1,0:T(8,128)(2,1)S(1)}, u32[]{:S(2)}, u32[]{:S(2)}) %all-to-all-start.4) | async-done | bytes 327712 | tf_op jit(solution)/shard_map/all_to_all | solution.py:29
  136.6 0.7 copy-done.3
  137.3 13.6 %moved.1.refs_0_ = bf16[2048,128]{1,0:T(8,128)(2,1)} custom-call(s32[40]{0:T(128)} %select_reduce_fusion.1.where_ref, s32[2]{0:T(128)} %pad_add_fusion.1.bound_ref, bf16[8,2,16,640]{3,2,1,0:T(8,128)(2,1)} %copy-done.3, bf16[8,128,256]{2,1,0:T(8,128)(2,1)} %pad_maximum_fusion.1.refs_0_, bf16[8,128,256]{2,1,0:T(8,128)(2,1)} %collective-permute-done.3.refs_1_, ...), custom_call_target="tpu_custom_call" | custom-call | tf_op jit(solution)/shard_map/moved/pallas_call | solution.py:85
  150.9 0.6 collective-permute-start.10
  151.5 0.9 collective-permute-start.13
  152.4 2.4 collective-permute-start.14
  154.8 10.1 %collective-permute-done.10.refs_1_ = bf16[2048,128]{1,0:T(8,128)(2,1)} collective-permute-done((bf16[2048,128]{1,0:T(8,128)(2,1)}, bf16[2048,128]{1,0:T(8,128)(2,1)}, u32[]{:S(2)}, u32[]{:S(2)}) %collective-permute-start.10) | collective-permute-done | bytes 524320 | tf_op jit(solution)/shard_map/ppermute | solution.py:266
  165.1 1.8 collective-permute-start.23
  167.4 10.6 %partial.2 = (bf16[288,512]{1,0:T(8,128)(2,1)}, bf16[288,512]{1,0:T(8,128)(2,1)}, bf16[288,512]{1,0:T(8,128)(2,1)}, bf16[288,512]{1,0:T(8,128)(2,1)}, bf16[288,5...) custom-call(s32[8]{0:T(128)} %stack.85.dest_ref, ...), custom_call_target="tpu_custom_call" | custom-call | tf_op jit(solution)/shard_map/partial/pallas_call | solution.py:131
  178.1 3.1 %collective-permute-start.25 = (bf16[2048,128]{1,0:T(8,128)(2,1)S(1)}, bf16[2048,128]{1,0:T(8,128)(2,1)S(1)}, u32[]{:S(2)}, u32[]{:S(2)}) collective-permute-start(bf16[2048,128]{1,0:T(8,128)(2,1)S(1)} %collective-permute-done.11.refs_1_), channel_id=1, source_target_pairs={{0,3},{1,0},{2,1},{3,2},{4,7},{5,4},{6,5},{7,6},{8,11},{9,8},{10,9... | collective-permute-start | bytes 1572872 | tf_op jit(solution)/shard_map/ppermute | solution.py:274
  181.1 0.7 collective-permute-start.15
  181.9 2.6 %collective-permute-start.16 = (bf16[288,512]{1,0:T(8,128)(2,1)}, bf16[288,512]{1,0:T(8,128)(2,1)}, u32[]{:S(2)}, u32[]{:S(2)}) collective-permute-start(bf16[288,512]{1,0:T(8,128)(2,1)} %get-tuple-element.77), channel_id=1, source_target_pairs={{0,16},{16,32},{32,48},{48,0},{64,80},{80,96},{96,112},{112,64},{1... | collective-permute-start | bytes 884744 | tf_op jit(solution)/shard_map/ppermute | solution.py:281
  184.5 0.6 collective-permute-start.17
  185.1 5.2 %collective-permute-done.24.refs_2_ = bf16[2048,128]{1,0:T(8,128)(2,1)} collective-permute-done((bf16[2048,128]{1,0:T(8,128)(2,1)}, bf16[2048,128]{1,0:T(8,128)(2,1)}, u32[]{:S(2)}, u32[]{:S(2)}) %collective-permute-start.24) | collective-permute-done | bytes 524320 | tf_op jit(solution)/shard_map/ppermute | solution.py:271
  190.3 1.9 collective-permute-start.18
  192.2 0.8 copy-done.6
  193.0 3.7 %collective-permute-start.19 = (bf16[288,512]{1,0:T(8,128)(2,1)}, bf16[288,512]{1,0:T(8,128)(2,1)}, u32[]{:S(2)}, u32[]{:S(2)}) collective-permute-start(bf16[288,512]{1,0:T(8,128)(2,1)} %get-tuple-element.82), channel_id=1, source_target_pairs={{0,80},{16,96},{32,112},{48,64},{64,16},{80,32},{96,48},{112,0},{1... | collective-permute-start | bytes 884744 | tf_op jit(solution)/shard_map/ppermute | solution.py:281
  196.6 10.6 %partial.3 = (bf16[288,512]{1,0:T(8,128)(2,1)}, bf16[288,512]{1,0:T(8,128)(2,1)}, bf16[288,512]{1,0:T(8,128)(2,1)}, bf16[288,512]{1,0:T(8,128)(2,1)}, bf16[288,5...) custom-call(s32[8]{0:T(128)} %stack.85.dest_ref, ...), custom_call_target="tpu_custom_call" | custom-call | tf_op jit(solution)/shard_map/partial/pallas_call | solution.py:131
  207.3 2.0 collective-permute-start.20
  209.3 2.1 collective-permute-start.21
  211.4 1.3 collective-permute-start.26
  213.0 3.0 %collective-permute-start.28 = (bf16[288,512]{1,0:T(8,128)(2,1)}, bf16[288,512]{1,0:T(8,128)(2,1)S(1)}, u32[]{:S(2)}, u32[]{:S(2)}) collective-permute-start(bf16[288,512]{1,0:T(8,128)(2,1)} %get-tuple-element.95), channel_id=1, source_target_pairs={{0,48},{16,0},{32,16},{48,32},{64,112},{80,64},{96,80},{112,96},{1... | collective-permute-start | bytes 884744 | tf_op jit(solution)/shard_map/ppermute | solution.py:281
  216.0 1.5 convert_add_fusion.2
  217.5 1.8 collective-permute-done.20
  219.3 2.3 collective-permute-start.29
  221.6 4.0 %collective-permute-done.21 = bf16[288,512]{1,0:T(8,128)(2,1)S(1)} collective-permute-done((bf16[288,512]{1,0:T(8,128)(2,1)}, bf16[288,512]{1,0:T(8,128)(2,1)S(1)}, u32[]{:S(2)}, u32[]{:S(2)}) %collective-permute-start.21) | collective-permute-done | bytes 294944 | tf_op jit(solution)/shard_map/ppermute | solution.py:281
  225.6 0.9 collective-permute-start.30
  226.5 5.2 %collective-permute-done.26 = bf16[288,512]{1,0:T(8,128)(2,1)} collective-permute-done((bf16[288,512]{1,0:T(8,128)(2,1)}, bf16[288,512]{1,0:T(8,128)(2,1)}, u32[]{:S(2)}, u32[]{:S(2)}) %collective-permute-start.26) | collective-permute-done | bytes 294944 | tf_op jit(solution)/shard_map/ppermute | solution.py:281
  231.7 7.5 %collective-permute-done.27 = bf16[288,512]{1,0:T(8,128)(2,1)} collective-permute-done((bf16[288,512]{1,0:T(8,128)(2,1)}, bf16[288,512]{1,0:T(8,128)(2,1)}, u32[]{:S(2)}, u32[]{:S(2)}) %collective-permute-start.27) | collective-permute-done | bytes 294944 | tf_op jit(solution)/shard_map/ppermute | solution.py:281
  239.2 2.6 %collective-permute-start.32 = (bf16[288,512]{1,0:T(8,128)(2,1)}, bf16[288,512]{1,0:T(8,128)(2,1)S(1)}, u32[]{:S(2)}, u32[]{:S(2)}) collective-permute-start(bf16[288,512]{1,0:T(8,128)(2,1)} %get-tuple-element.101), channel_id=1, source_target_pairs={{0,64},{16,80},{32,96},{48,112},{64,0},{80,16},{96,32},{112,48},{1... | collective-permute-start | bytes 884744 | tf_op jit(solution)/shard_map/ppermute | solution.py:281
  241.8 1.0 add_add_fusion.3
  242.9 1.3 convert_add_fusion
  244.2 5.5 %collective-permute-done.32 = bf16[288,512]{1,0:T(8,128)(2,1)S(1)} collective-permute-done((bf16[288,512]{1,0:T(8,128)(2,1)}, bf16[288,512]{1,0:T(8,128)(2,1)S(1)}, u32[]{:S(2)}, u32[]{:S(2)}) %collective-permute-start.32) | collective-permute-done | bytes 294944 | tf_op jit(solution)/shard_map/ppermute | solution.py:281
  249.9 2.0 add_add_fusion
  251.8 3.0 %finish.1 = f32[144,2,1024]{2,1,0:T(2,128)} custom-call(s32[1]{0:T(128)} %bitcast.core_ref, s32[8]{0:T(128)} %stack.76.place_ref, f32[144,512]{1,0:T(8,128)} %get-tuple-element.126.refs_0_, f32[144,512]{1,0:T(8,128)} %collective-permute-done.22.refs_1_, f32[144,512]{1,0:T(8,128)} %get-tuple-element.125.refs_2_, f32[144,512]{1,0:T(8,128)} %collective-permute-done.33.refs_3_), custom_call_target="tpu_custom_call" | custom-call | tf_op jit(solution)/shard_map/finish/pallas_call | solution.py:160
  (99 shorter events, 6.1 us)
Async XLA Ops:
  0.0 19.4 %copy-start = (bf16[768,1408]{1,0:T(8,128)(2,1)S(1)}, bf16[768,1408]{1,0:T(8,128)(2,1)}, u32[]{:S(2)}) copy-start(bf16[768,1408]{1,0:T(8,128)(2,1)} %param.9) | copy-start | bytes 6488068
  2.4 15.8 %all-to-all-start = ((s32[16,8,128]{2,1,0:T(8,128)}), s32[16,8,128]{2,1,0:T(8,128)S(1)}, u32[]{:S(2)}, u32[]{:S(2)}) async-start(s32[16,8,128]{2,1,0:T(8,128)} %broadcast_in_dim_broadcast_in_dim_broadcast_in_dim.2), calls=%async_computation | async-start | bytes 131072 | tf_op jit(solution)/shard_map/all_to_all | solution.py:29
  19.4 1.8 copy-start.9
  21.1 1.7 copy-start.1
  22.9 2.8 %collective-permute-start = (bf16[640,768]{1,0:T(8,128)(2,1)}, bf16[640,768]{1,0:T(8,128)(2,1)S(1)}, u32[]{:S(2)}, u32[]{:S(2)}) collective-permute-start(bf16[640,768]{1,0:T(8,128)(2,1)} %broadcast_select_fusion.2), channel_id=1, source_target_pairs={{0,8},{8,0},{1,9},{9,1},{2,10},{10,2},{3,11},{11,3},{4,12},{12,4},... | collective-permute-start | bytes 2949128 | tf_op jit(solution)/shard_map/ppermute | solution.py:216
  28.4 3.7 %slice-start = ((bf16[2304,4,256]{2,1,0:T(4,128)(2,1)}), bf16[128,4,256]{2,1,0:T(4,128)(2,1)S(1)}, s32[]{:S(2)}) async-start(bf16[2304,4,256]{2,1,0:T(4,128)(2,1)} %param.15), calls=%async_computation.5 | async-start | bytes 524288 | tf_op jit(solution)/shard_map/slice | solution.py:176
  28.4 25.0 %all-to-all-start.1 = ((bf16[8,80,768]{2,1,0:T(8,128)(2,1)}), bf16[8,80,768]{2,1,0:T(8,128)(2,1)S(1)}, u32[]{:S(2)}, u32[]{:S(2)}) async-start(bf16[8,80,768]{2,1,0:T(8,128)(2,1)} %bitcast.22), calls=%async_computation.1 | async-start | bytes 1966080 | tf_op jit(solution)/shard_map/all_to_all | solution.py:226
  32.1 20.5 %collective-permute-start.1 = (bf16[4,128,256]{2,1,0:T(8,128)(2,1)S(1)}, bf16[4,128,256]{2,1,0:T(8,128)(2,1)S(1)}, u32[]{:S(2)}, u32[]{:S(2)}) collective-permute-start(bf16[4,128,256]{2,1,0:T(8,128)(2,1)S(1)} %bitcast.53), channel_id=1, source_target_pairs={{0,64},{64,0},{1,65},{65,1},{2,66},{66,2},{3,67},{67,3},{4,68},{68... | collective-permute-start | bytes 786440 | tf_op jit(solution)/shard_map/ppermute | solution.py:177
  35.7 6.0 %copy-start.10 = (f32[2]{0:T(128)S(1)}, f32[2]{0:T(128)}, u32[]{:S(2)}) copy-start(f32[2]{0:T(128)} %param.12) | copy-start | bytes 28
  53.4 22.1 %copy-start.11 = (f32[128]{0:T(128)S(1)}, f32[128]{0:T(128)}, u32[]{:S(2)}) copy-start(f32[128]{0:T(128)} %param.10) | copy-start | bytes 1540
  53.4 22.8 %copy-start.8 = (f32[1408]{0:T(1024)S(1)}, f32[1408]{0:T(1024)}, u32[]{:S(2)}) copy-start(f32[1408]{0:T(1024)} %param.11) | copy-start | bytes 16900
  73.7 2.7 %collective-permute-start.2 = (bf16[640,768]{1,0:T(8,128)(2,1)S(1)}, bf16[640,768]{1,0:T(8,128)(2,1)}, u32[]{:S(2)}, u32[]{:S(2)}) collective-permute-start(bf16[640,768]{1,0:T(8,128)(2,1)S(1)} %bitcast.51), channel_id=1, source_target_pairs={{0,8},{8,0},{1,9},{9,1},{2,10},{10,2},{3,11},{11,3},{4,12},{12,4},... | collective-permute-start | bytes 2949128 | tf_op jit(solution)/shard_map/ppermute | solution.py:236
  79.0 16.9 %copy-start.2 = (bf16[8,128,256]{2,1,0:T(8,128)(2,1)S(1)}, bf16[8,128,256]{2,1,0:T(8,128)(2,1)}, u32[]{:S(2)}) copy-start(bf16[8,128,256]{2,1,0:T(8,128)(2,1)} %pad_maximum_fusion.1.refs_0_) | copy-start | bytes 1572868
  95.9 71.5 %collective-permute-start.12 = (bf16[2304,1024]{1,0:T(8,128)(2,1)}, bf16[2304,1024]{1,0:T(8,128)(2,1)}, u32[]{:S(2)}, u32[]{:S(2)}) collective-permute-start(bf16[2304,1024]{1,0:T(8,128)(2,1)} %bitcast.47), channel_id=1, source_target_pairs={{0,8},{8,0},{1,9},{9,1},{2,10},{10,2},{3,11},{11,3},{4,12},{12,4},... | collective-permute-start | bytes 14155784 | tf_op jit(solution)/shard_map/ppermute | solution.py:258
  96.0 26.9 %collective-permute-start.3 = (bf16[8,128,256]{2,1,0:T(8,128)(2,1)S(1)}, bf16[8,128,256]{2,1,0:T(8,128)(2,1)}, u32[]{:S(2)}, u32[]{:S(2)}) collective-permute-start(bf16[8,128,256]{2,1,0:T(8,128)(2,1)S(1)} %copy-done.2), channel_id=1, source_target_pairs={{0,16},{16,32},{32,48},{48,0},{1,17},{17,33},{33,49},{49,1},{2,18}... | collective-permute-start | bytes 1572872 | tf_op jit(solution)/shard_map/ppermute | solution.py:232
  96.4 26.5 %collective-permute-start.4 = (bf16[8,128,256]{2,1,0:T(8,128)(2,1)S(1)}, bf16[8,128,256]{2,1,0:T(8,128)(2,1)}, u32[]{:S(2)}, u32[]{:S(2)}) collective-permute-start(bf16[8,128,256]{2,1,0:T(8,128)(2,1)S(1)} %copy-done.2), channel_id=1, source_target_pairs={{0,32},{16,48},{32,0},{48,16},{1,33},{17,49},{33,1},{49,17},{2,34}... | collective-permute-start | bytes 1572872 | tf_op jit(solution)/shard_map/ppermute | solution.py:232
  98.5 25.0 %collective-permute-start.5 = (bf16[8,128,256]{2,1,0:T(8,128)(2,1)S(1)}, bf16[8,128,256]{2,1,0:T(8,128)(2,1)}, u32[]{:S(2)}, u32[]{:S(2)}) collective-permute-start(bf16[8,128,256]{2,1,0:T(8,128)(2,1)S(1)} %copy-done.2), channel_id=1, source_target_pairs={{0,48},{16,0},{32,16},{48,32},{1,49},{17,1},{33,17},{49,33},{2,50}... | collective-permute-start | bytes 1572872 | tf_op jit(solution)/shard_map/ppermute | solution.py:232
  99.6 31.5 %collective-permute-start.6 = (bf16[8,128,256]{2,1,0:T(8,128)(2,1)S(1)}, bf16[8,128,256]{2,1,0:T(8,128)(2,1)}, u32[]{:S(2)}, u32[]{:S(2)}) collective-permute-start(bf16[8,128,256]{2,1,0:T(8,128)(2,1)S(1)} %copy-done.2), channel_id=1, source_target_pairs={{0,8},{8,0},{1,9},{9,1},{2,10},{10,2},{3,11},{11,3},{4,12},{12,4},... | collective-permute-start | bytes 1572872 | tf_op jit(solution)/shard_map/ppermute | solution.py:233
  122.9 8.2 %collective-permute-start.7 = (bf16[8,128,256]{2,1,0:T(8,128)(2,1)}, bf16[8,128,256]{2,1,0:T(8,128)(2,1)}, u32[]{:S(2)}, u32[]{:S(2)}) collective-permute-start(bf16[8,128,256]{2,1,0:T(8,128)(2,1)} %collective-permute-done.3.refs_1_), channel_id=1, source_target_pairs={{0,8},{8,0},{1,9},{9,1},{2,10},{10,2},{3,11},{11,3},{4,12},{12,4},... | collective-permute-start | bytes 1572872 | tf_op jit(solution)/shard_map/ppermute | solution.py:233
  122.9 8.2 %collective-permute-start.8 = (bf16[8,128,256]{2,1,0:T(8,128)(2,1)}, bf16[8,128,256]{2,1,0:T(8,128)(2,1)}, u32[]{:S(2)}, u32[]{:S(2)}) collective-permute-start(bf16[8,128,256]{2,1,0:T(8,128)(2,1)} %collective-permute-done.4.refs_2_), channel_id=1, source_target_pairs={{0,8},{8,0},{1,9},{9,1},{2,10},{10,2},{3,11},{11,3},{4,12},{12,4},... | collective-permute-start | bytes 1572872 | tf_op jit(solution)/shard_map/ppermute | solution.py:233
  123.5 7.6 %collective-permute-start.9 = (bf16[8,128,256]{2,1,0:T(8,128)(2,1)}, bf16[8,128,256]{2,1,0:T(8,128)(2,1)}, u32[]{:S(2)}, u32[]{:S(2)}) collective-permute-start(bf16[8,128,256]{2,1,0:T(8,128)(2,1)} %collective-permute-done.5.refs_3_), channel_id=1, source_target_pairs={{0,8},{8,0},{1,9},{9,1},{2,10},{10,2},{3,11},{11,3},{4,12},{12,4},... | collective-permute-start | bytes 1572872 | tf_op jit(solution)/shard_map/ppermute | solution.py:233
  124.2 12.3 %all-to-all-start.4 = ((bf16[8,2,16,640]{3,2,1,0:T(8,128)(2,1)}), bf16[8,2,16,640]{3,2,1,0:T(8,128)(2,1)S(1)}, u32[]{:S(2)}, u32[]{:S(2)}) async-start(bf16[8,2,16,640]{3,2,1,0:T(8,128)(2,1)} %broadcast_in_dim.111), calls=%async_computation.4 | async-start | bytes 655360 | tf_op jit(solution)/shard_map/all_to_all | solution.py:29
  136.6 0.7 copy-start.3
  150.9 14.0 %collective-permute-start.10 = (bf16[2048,128]{1,0:T(8,128)(2,1)}, bf16[2048,128]{1,0:T(8,128)(2,1)}, u32[]{:S(2)}, u32[]{:S(2)}) collective-permute-start(bf16[2048,128]{1,0:T(8,128)(2,1)} %moved.1.refs_0_), channel_id=1, source_target_pairs={{0,4},{4,0},{1,5},{5,1},{2,6},{6,2},{3,7},{7,3},{8,12},{12,8},{9,1... | collective-permute-start | bytes 1572872 | tf_op jit(solution)/shard_map/ppermute | solution.py:266
  151.5 15.4 %collective-permute-start.13 = (bf16[2048,128]{1,0:T(8,128)(2,1)}, bf16[2048,128]{1,0:T(8,128)(2,1)}, u32[]{:S(2)}, u32[]{:S(2)}) collective-permute-start(bf16[2048,128]{1,0:T(8,128)(2,1)} %moved.1.refs_0_), channel_id=1, source_target_pairs={{0,1},{1,2},{2,3},{3,0},{4,5},{5,6},{6,7},{7,4},{8,9},{9,10},{10,1... | collective-permute-start | bytes 1572872 | tf_op jit(solution)/shard_map/ppermute | solution.py:267
  152.4 15.0 %collective-permute-start.14 = (bf16[2048,128]{1,0:T(8,128)(2,1)}, bf16[2048,128]{1,0:T(8,128)(2,1)}, u32[]{:S(2)}, u32[]{:S(2)}) collective-permute-start(bf16[2048,128]{1,0:T(8,128)(2,1)} %moved.1.refs_0_), channel_id=1, source_target_pairs={{0,3},{1,0},{2,1},{3,2},{4,7},{5,4},{6,5},{7,6},{8,11},{9,8},{10,9... | collective-permute-start | bytes 1572872 | tf_op jit(solution)/shard_map/ppermute | solution.py:268
  164.8 13.2 %collective-permute-start.11 = (bf16[2048,128]{1,0:T(8,128)(2,1)}, bf16[2048,128]{1,0:T(8,128)(2,1)S(1)}, u32[]{:S(2)}, u32[]{:S(2)}) collective-permute-start(bf16[2048,128]{1,0:T(8,128)(2,1)} %collective-permute-done.10.refs_1_), channel_id=1, source_target_pairs={{0,3},{1,0},{2,1},{3,2},{4,7},{5,4},{6,5},{7,6},{8,11},{9,8},{10,9... | collective-permute-start | bytes 1572872 | tf_op jit(solution)/shard_map/ppermute | solution.py:270
  165.1 19.4 %collective-permute-start.23 = (bf16[2048,128]{1,0:T(8,128)(2,1)}, bf16[2048,128]{1,0:T(8,128)(2,1)S(1)}, u32[]{:S(2)}, u32[]{:S(2)}) collective-permute-start(bf16[2048,128]{1,0:T(8,128)(2,1)} %collective-permute-done.10.refs_1_), channel_id=1, source_target_pairs={{0,1},{1,2},{2,3},{3,0},{4,5},{5,6},{6,7},{7,4},{8,9},{9,10},{10,1... | collective-permute-start | bytes 1572872 | tf_op jit(solution)/shard_map/ppermute | solution.py:269
  166.9 23.5 %collective-permute-start.24 = (bf16[2048,128]{1,0:T(8,128)(2,1)}, bf16[2048,128]{1,0:T(8,128)(2,1)}, u32[]{:S(2)}, u32[]{:S(2)}) collective-permute-start(bf16[2048,128]{1,0:T(8,128)(2,1)} %collective-permute-done.13.refs_2_), channel_id=1, source_target_pairs={{0,1},{1,2},{2,3},{3,0},{4,5},{5,6},{6,7},{7,4},{8,9},{9,10},{10,1... | collective-permute-start | bytes 1572872 | tf_op jit(solution)/shard_map/ppermute | solution.py:271
  178.1 18.6 %copy-start.4 = (bf16[2048,128]{1,0:T(8,128)(2,1)}, bf16[2048,128]{1,0:T(8,128)(2,1)S(1)}, u32[]{:S(2)}) copy-start(bf16[2048,128]{1,0:T(8,128)(2,1)S(1)} %collective-permute-done.11.refs_1_) | copy-start | bytes 1572868
  178.1 14.1 %collective-permute-start.25 = (bf16[2048,128]{1,0:T(8,128)(2,1)S(1)}, bf16[2048,128]{1,0:T(8,128)(2,1)S(1)}, u32[]{:S(2)}, u32[]{:S(2)}) collective-permute-start(bf16[2048,128]{1,0:T(8,128)(2,1)S(1)} %collective-permute-done.11.refs_1_), channel_id=1, source_target_pairs={{0,3},{1,0},{2,1},{3,2},{4,7},{5,4},{6,5},{7,6},{8,11},{9,8},{10,9... | collective-permute-start | bytes 1572872 | tf_op jit(solution)/shard_map/ppermute | solution.py:274
  181.1 26.1 %collective-permute-start.15 = (bf16[288,512]{1,0:T(8,128)(2,1)}, bf16[288,512]{1,0:T(8,128)(2,1)}, u32[]{:S(2)}, u32[]{:S(2)}) collective-permute-start(bf16[288,512]{1,0:T(8,128)(2,1)} %get-tuple-element.76), channel_id=1, source_target_pairs={{0,32},{16,48},{32,0},{48,16},{64,96},{80,112},{96,64},{112,80},{1... | collective-permute-start | bytes 884744 | tf_op jit(solution)/shard_map/ppermute | solution.py:281
  181.9 27.4 %collective-permute-start.16 = (bf16[288,512]{1,0:T(8,128)(2,1)}, bf16[288,512]{1,0:T(8,128)(2,1)}, u32[]{:S(2)}, u32[]{:S(2)}) collective-permute-start(bf16[288,512]{1,0:T(8,128)(2,1)} %get-tuple-element.77), channel_id=1, source_target_pairs={{0,16},{16,32},{32,48},{48,0},{64,80},{80,96},{96,112},{112,64},{1... | collective-permute-start | bytes 884744 | tf_op jit(solution)/shard_map/ppermute | solution.py:281
  184.5 12.2 %copy-start.5 = (bf16[2048,128]{1,0:T(8,128)(2,1)}, bf16[2048,128]{1,0:T(8,128)(2,1)S(1)}, u32[]{:S(2)}) copy-start(bf16[2048,128]{1,0:T(8,128)(2,1)S(1)} %collective-permute-done.23.refs_0_) | copy-start | bytes 1572868
  184.5 26.9 %collective-permute-start.17 = (bf16[288,512]{1,0:T(8,128)(2,1)}, bf16[288,512]{1,0:T(8,128)(2,1)}, u32[]{:S(2)}, u32[]{:S(2)}) collective-permute-start(bf16[288,512]{1,0:T(8,128)(2,1)} %get-tuple-element.78), channel_id=1, source_target_pairs={{0,48},{16,0},{32,16},{48,32},{64,112},{80,64},{96,80},{112,96},{1... | collective-permute-start | bytes 884744 | tf_op jit(solution)/shard_map/ppermute | solution.py:281
  190.3 22.4 %collective-permute-start.18 = (bf16[288,512]{1,0:T(8,128)(2,1)}, bf16[288,512]{1,0:T(8,128)(2,1)S(1)}, u32[]{:S(2)}, u32[]{:S(2)}) collective-permute-start(bf16[288,512]{1,0:T(8,128)(2,1)} %get-tuple-element.81), channel_id=1, source_target_pairs={{0,96},{16,112},{32,64},{48,80},{64,32},{80,48},{96,0},{112,16},{1... | collective-permute-start | bytes 884744 | tf_op jit(solution)/shard_map/ppermute | solution.py:281
  192.2 0.8 copy-start.6
  193.0 20.0 %collective-permute-start.19 = (bf16[288,512]{1,0:T(8,128)(2,1)}, bf16[288,512]{1,0:T(8,128)(2,1)}, u32[]{:S(2)}, u32[]{:S(2)}) collective-permute-start(bf16[288,512]{1,0:T(8,128)(2,1)} %get-tuple-element.82), channel_id=1, source_target_pairs={{0,80},{16,96},{32,112},{48,64},{64,16},{80,32},{96,48},{112,0},{1... | collective-permute-start | bytes 884744 | tf_op jit(solution)/shard_map/ppermute | solution.py:281
  207.3 12.0 %collective-permute-start.20 = (bf16[288,512]{1,0:T(8,128)(2,1)}, bf16[288,512]{1,0:T(8,128)(2,1)S(1)}, u32[]{:S(2)}, u32[]{:S(2)}) collective-permute-start(bf16[288,512]{1,0:T(8,128)(2,1)} %get-tuple-element.83), channel_id=1, source_target_pairs={{0,112},{16,64},{32,80},{48,96},{64,48},{80,0},{96,16},{112,32},{1... | collective-permute-start | bytes 884744 | tf_op jit(solution)/shard_map/ppermute | solution.py:281
  209.3 16.3 %collective-permute-start.21 = (bf16[288,512]{1,0:T(8,128)(2,1)}, bf16[288,512]{1,0:T(8,128)(2,1)S(1)}, u32[]{:S(2)}, u32[]{:S(2)}) collective-permute-start(bf16[288,512]{1,0:T(8,128)(2,1)} %get-tuple-element.84), channel_id=1, source_target_pairs={{0,64},{16,80},{32,96},{48,112},{64,0},{80,16},{96,32},{112,48},{1... | collective-permute-start | bytes 884744 | tf_op jit(solution)/shard_map/ppermute | solution.py:281
  211.4 20.3 %collective-permute-start.26 = (bf16[288,512]{1,0:T(8,128)(2,1)}, bf16[288,512]{1,0:T(8,128)(2,1)}, u32[]{:S(2)}, u32[]{:S(2)}) collective-permute-start(bf16[288,512]{1,0:T(8,128)(2,1)} %get-tuple-element.93), channel_id=1, source_target_pairs={{0,32},{16,48},{32,0},{48,16},{64,96},{80,112},{96,64},{112,80},{1... | collective-permute-start | bytes 884744 | tf_op jit(solution)/shard_map/ppermute | solution.py:281
  212.8 26.4 %collective-permute-start.27 = (bf16[288,512]{1,0:T(8,128)(2,1)}, bf16[288,512]{1,0:T(8,128)(2,1)}, u32[]{:S(2)}, u32[]{:S(2)}) collective-permute-start(bf16[288,512]{1,0:T(8,128)(2,1)} %get-tuple-element.94), channel_id=1, source_target_pairs={{0,16},{16,32},{32,48},{48,0},{64,80},{80,96},{96,112},{112,64},{1... | collective-permute-start | bytes 884744 | tf_op jit(solution)/shard_map/ppermute | solution.py:281
  213.0 29.9 %copy-start.7 = (bf16[288,512]{1,0:T(8,128)(2,1)S(1)}, bf16[288,512]{1,0:T(8,128)(2,1)}, u32[]{:S(2)}) copy-start(bf16[288,512]{1,0:T(8,128)(2,1)} %get-tuple-element.96) | copy-start | bytes 884740
  213.0 29.7 %collective-permute-start.28 = (bf16[288,512]{1,0:T(8,128)(2,1)}, bf16[288,512]{1,0:T(8,128)(2,1)S(1)}, u32[]{:S(2)}, u32[]{:S(2)}) collective-permute-start(bf16[288,512]{1,0:T(8,128)(2,1)} %get-tuple-element.95), channel_id=1, source_target_pairs={{0,48},{16,0},{32,16},{48,32},{64,112},{80,64},{96,80},{112,96},{1... | collective-permute-start | bytes 884744 | tf_op jit(solution)/shard_map/ppermute | solution.py:281
  219.3 24.8 %collective-permute-start.29 = (bf16[288,512]{1,0:T(8,128)(2,1)}, bf16[288,512]{1,0:T(8,128)(2,1)S(1)}, u32[]{:S(2)}, u32[]{:S(2)}) collective-permute-start(bf16[288,512]{1,0:T(8,128)(2,1)} %get-tuple-element.98), channel_id=1, source_target_pairs={{0,96},{16,112},{32,64},{48,80},{64,32},{80,48},{96,0},{112,16},{1... | collective-permute-start | bytes 884744 | tf_op jit(solution)/shard_map/ppermute | solution.py:281
  225.6 18.5 %collective-permute-start.30 = (bf16[288,512]{1,0:T(8,128)(2,1)}, bf16[288,512]{1,0:T(8,128)(2,1)S(1)}, u32[]{:S(2)}, u32[]{:S(2)}) collective-permute-start(bf16[288,512]{1,0:T(8,128)(2,1)} %get-tuple-element.99), channel_id=1, source_target_pairs={{0,80},{16,96},{32,112},{48,64},{64,16},{80,32},{96,48},{112,0},{1... | collective-permute-start | bytes 884744 | tf_op jit(solution)/shard_map/ppermute | solution.py:281
  231.7 12.4 %collective-permute-start.31 = (bf16[288,512]{1,0:T(8,128)(2,1)}, bf16[288,512]{1,0:T(8,128)(2,1)S(1)}, u32[]{:S(2)}, u32[]{:S(2)}) collective-permute-start(bf16[288,512]{1,0:T(8,128)(2,1)} %get-tuple-element.100), channel_id=1, source_target_pairs={{0,112},{16,64},{32,80},{48,96},{64,48},{80,0},{96,16},{112,32},{1... | collective-permute-start | bytes 884744 | tf_op jit(solution)/shard_map/ppermute | solution.py:281
  239.2 10.5 %collective-permute-start.32 = (bf16[288,512]{1,0:T(8,128)(2,1)}, bf16[288,512]{1,0:T(8,128)(2,1)S(1)}, u32[]{:S(2)}, u32[]{:S(2)}) collective-permute-start(bf16[288,512]{1,0:T(8,128)(2,1)} %get-tuple-element.101), channel_id=1, source_target_pairs={{0,64},{16,80},{32,96},{48,112},{64,0},{80,16},{96,32},{112,48},{1... | collective-permute-start | bytes 884744 | tf_op jit(solution)/shard_map/ppermute | solution.py:281
  242.8 9.1 %collective-permute-start.22 = (f32[144,512]{1,0:T(8,128)S(1)}, f32[144,512]{1,0:T(8,128)}, u32[]{:S(2)}, u32[]{:S(2)}) collective-permute-start(f32[144,512]{1,0:T(8,128)S(1)} %add_add_fusion.3), channel_id=1, source_target_pairs={{0,8},{8,0},{1,9},{9,1},{2,10},{10,2},{3,11},{11,3},{4,12},{12,4},... | collective-permute-start | bytes 884744 | tf_op jit(solution)/shard_map/ppermute | solution.py:293
  249.8 2.1 collective-permute-start.33
